TPU v7x, 32 devices: a whole 2x2x4 slice. The times are simulated.
32 devices in a mesh: seq: 8 (over z, y), head: 4 (over x, core).
Axes of the slice: x: 2, y: 2, z: 4, core: 2. Of those that a mesh axis runs over, the one named last changes fastest.
Arguments:
- layer_input: bfloat16 [4096, 768], P('seq', 'head'), may hold values from -6 to 6
- ln1_gain: float32 [768], replicated, may hold values from 0.5 to 1.5
- ln1_bias: float32 [768], replicated, may hold values from -3 to 3
- w_query: bfloat16 [768, 768], P(None, 'head'), may hold values from -0.21875 to 0.21875
- b_query: float32 [768], P('head'), may hold values from -3 to 3
- w_key: bfloat16 [768, 768], P(None, 'head'), may hold values from -0.3125 to 0.3125
- w_value: bfloat16 [768, 768], P(None, 'head'), may hold values from -0.21875 to 0.21875
- b_value: float32 [768], P('head'), may hold values from -1.2 to 1.2
- sub_gain: float32 [768], P('head'), may hold values from 0.5 to 1.5
- sub_bias: float32 [768], P('head'), may hold values from -3 to 3
- w_out: bfloat16 [768, 768], P('head'), may hold values from -0.21875 to 0.21875
- b_out: float32 [768], replicated, may hold values from -3 to 3
- ln2_gain: float32 [768], replicated, may hold values from 0.5 to 1.5
- ln2_bias: float32 [768], replicated, may hold values from -3 to 3
- w_up: bfloat16 [768, 3072], P(None, 'head'), may hold values from -0.21875 to 0.21875
- b_up: float32 [3072], P('head'), may hold values from -3 to 3
- w_down: bfloat16 [3072, 768], P('head'), may hold values from -0.109375 to 0.109375
- b_down: float32 [768], replicated, may hold values from -3 to 3
- cotangent: bfloat16 [4096, 768], P('seq', 'head'), may hold values from -6 to 6
- row_lengths: int32 [6], replicated, may hold values from 1 to 3072, 4096 in all
Outputs:
- layer_output: bfloat16 [4096, 768], P('seq', 'head')
- grad_input: float32 [4096, 768], P('seq', 'head')
- grad_ln1_gain: float32 [768], replicated
- grad_ln1_bias: float32 [768], replicated
- grad_w_query: float32 [768, 768], P(None, 'head')
- grad_b_query: float32 [768], P('head')
- grad_w_key: float32 [768, 768], P(None, 'head')
- grad_w_value: float32 [768, 768], P(None, 'head')
- grad_b_value: float32 [768], P('head')
- grad_sub_gain: float32 [768], P('head')
- grad_sub_bias: float32 [768], P('head')
- grad_w_out: float32 [768, 768], P('head')
- grad_b_out: float32 [768], replicated
- grad_ln2_gain: float32 [768], replicated
- grad_ln2_bias: float32 [768], replicated
- grad_w_up: float32 [768, 3072], P(None, 'head')
- grad_b_up: float32 [3072], P('head')
- grad_w_down: float32 [3072, 768], P('head')
- grad_b_down: float32 [768], replicated
Inputs may be any that keep to these rules, and one draw needn't show every extreme that they name: `row_lengths`: the 6 row lengths sum to 4096, and the longest is exactly 3072.
All inputs are finite; a program needn't handle non-finite values.
Results may differ from a plain program's by a relative error of at most 0.018.
Values may be sent and summed in bfloat16 or wider, within the bound.
No kernel may reach another device: no remote copies, remote signals or barrier semaphores. Data moves between devices by JAX's collectives and lax.ppermute only.
A program may use at most 256 MiB of HBM per device.

v0:
```python
import math

import jax
import jax.numpy as jnp
from jax import lax
from jax.sharding import PartitionSpec as P

HEAD_DIM = 64
SEG = 2048


eps = 1e-05
segment_scales = (1, 2, 4, 8, 16)
dilation_steps = (1, 2, 4, 6, 12)


def layer_norm(inputs, norm_gain, norm_bias):
    center = inputs - jnp.mean(inputs, axis=-1, keepdims=True)
    spread = jnp.mean(center * center, axis=-1, keepdims=True)
    return center * lax.rsqrt(spread + eps) * norm_gain + norm_bias


def token_places(positions, lengths):
    row_ends = jnp.cumsum(lengths)
    starts = row_ends - lengths
    row_of = jnp.sum((positions[:, None] >= row_ends[None, :]).astype(jnp.int32), axis=1)
    onehot = (row_of[:, None] == jnp.arange(lengths.shape[0], dtype=jnp.int32)[None, :]).astype(
        jnp.int32
    )
    row_place = positions - jnp.sum(onehot * starts[None, :], axis=1)
    return (row_of, row_place)


def pattern_count(head_ids, query_row, query_place, key_row, key_place):
    allowed = (query_row[:, None] == key_row[None, :]) & (
        key_place[None, :] <= query_place[:, None]
    )
    counted = jnp.zeros((head_ids.shape[0], query_row.shape[0], key_row.shape[0]), jnp.float32)
    for scale_factor, step_size in zip(segment_scales, dilation_steps):
        seg_width = SEG * scale_factor
        same_seg = allowed & (query_place[:, None] // seg_width == key_place[None, :] // seg_width)
        offset = head_ids % step_size
        query_on = (query_place % seg_width % step_size)[None, :] == offset[:, None]
        key_on = (key_place % seg_width % step_size)[None, :] == offset[:, None]
        counted = counted + (same_seg[None] & query_on[:, :, None] & key_on[:, None, :]).astype(
            jnp.float32
        )
    return counted


def fold_keys(running, pieces, queries, head_ids, query_row, query_place, lengths, score_scale):
    key_rows, values = pieces
    piece_rows = key_rows.shape[0]
    block_rows = math.gcd(piece_rows, 2048)
    local_heads = queries.shape[0]
    key_blocks = key_rows.reshape(piece_rows // block_rows, block_rows, local_heads, -1)
    value_blocks = values.reshape(piece_rows // block_rows, block_rows, local_heads, -1)
    offsets = jnp.arange(piece_rows // block_rows, dtype=jnp.int32) * block_rows

    def advance(status, element):
        highest, totals, running_sum = status
        key_blk, value_blk, block_first = element
        key_row, key_place = token_places(
            block_first + jnp.arange(block_rows, dtype=jnp.int32), lengths
        )
        counted = pattern_count(head_ids, query_row, query_place, key_row, key_place)
        scores = (
            jnp.einsum("hqd,khd->hqk", queries, key_blk, preferred_element_type=jnp.float32)
            * score_scale
        )
        masked = jnp.where(counted > 0, scores, -1e30)
        new_high = jnp.maximum(highest, jnp.max(masked, axis=-1))
        weights = counted * jnp.exp(masked - new_high[..., None])
        factor = jnp.exp(highest - new_high)
        totals = totals * factor + jnp.sum(weights, axis=-1)
        running_sum = running_sum * factor[..., None] + jnp.einsum(
            "hqk,khd->hqd",
            weights.astype(jnp.bfloat16),
            value_blk,
            preferred_element_type=jnp.float32,
        )
        return ((new_high, totals, running_sum), None)

    running, unused = lax.scan(advance, running, (key_blocks, value_blocks, offsets))
    return running


def shards(
    layer_input,
    ln1_gain,
    ln1_bias,
    w_query,
    b_query,
    w_key,
    w_value,
    b_value,
    sub_gain,
    sub_bias,
    w_out,
    b_out,
    ln2_gain,
    ln2_bias,
    w_up,
    b_up,
    w_down,
    b_down,
    cotangent,
    row_lengths,
):
    rows_local = layer_input.shape[0]
    slice_width = layer_input.shape[1]
    head_share = w_query.shape[1]
    local_heads = head_share // HEAD_DIM
    head_pos = lax.axis_index("head")
    seq_pos = lax.axis_index("seq")
    full_width = head_share * lax.axis_size("head")
    score_scale = HEAD_DIM ** (-0.5)
    head_ids = head_pos * local_heads + jnp.arange(local_heads, dtype=jnp.int32)
    own_index = seq_pos * rows_local + jnp.arange(rows_local, dtype=jnp.int32)
    query_row, query_place = token_places(own_index, row_lengths)
    input_whole = lax.all_gather(layer_input, "head", axis=1, tiled=True).astype(jnp.float32)
    normed = layer_norm(input_whole, ln1_gain, ln1_bias).astype(jnp.bfloat16)
    queries = (jnp.dot(normed, w_query, preferred_element_type=jnp.float32) + b_query).astype(
        jnp.bfloat16
    )
    key_rows = jnp.dot(normed, w_key, preferred_element_type=jnp.float32).astype(jnp.bfloat16)
    values = (jnp.dot(normed, w_value, preferred_element_type=jnp.float32) + b_value).astype(
        jnp.bfloat16
    )
    query_heads = queries.reshape(rows_local, local_heads, HEAD_DIM).transpose(1, 0, 2)
    start_state = (
        jnp.full((local_heads, rows_local), -1e30, jnp.float32),
        jnp.zeros((local_heads, rows_local), jnp.float32),
        jnp.zeros((local_heads, rows_local, HEAD_DIM), jnp.float32),
    )
    highest, totals, running_sum = fold_keys(
        start_state,
        (
            lax.all_gather(key_rows, "seq", axis=0, tiled=True),
            lax.all_gather(values, "seq", axis=0, tiled=True),
        ),
        query_heads,
        head_ids,
        query_row,
        query_place,
        row_lengths,
        score_scale,
    )
    attended = running_sum / totals[..., None]
    log_total = highest + jnp.log(totals)
    mixed_heads = attended.transpose(1, 0, 2).reshape(rows_local, head_share)
    row_sum, row_square = lax.psum(
        (jnp.sum(mixed_heads, axis=1), jnp.sum(mixed_heads * mixed_heads, axis=1)), "head"
    )
    mean_value = row_sum / full_width
    inv_std = lax.rsqrt(row_square / full_width - mean_value * mean_value + eps)
    centered = (mixed_heads - mean_value[:, None]) * inv_std[:, None]
    sub_out = (centered * sub_gain + sub_bias).astype(jnp.bfloat16)
    projected = lax.psum_scatter(
        jnp.dot(sub_out, w_out, preferred_element_type=jnp.float32).astype(jnp.bfloat16),
        "head",
        scatter_dimension=1,
        tiled=True,
    ).astype(jnp.float32)
    out_bias_share = lax.dynamic_slice_in_dim(b_out, head_pos * slice_width, slice_width, 0)
    middle = layer_input.astype(jnp.float32) + (projected + out_bias_share)
    middle_whole = lax.all_gather(middle.astype(jnp.bfloat16), "head", axis=1, tiled=True).astype(
        middle.dtype
    )
    normed_mid = layer_norm(middle_whole, ln2_gain, ln2_bias).astype(jnp.bfloat16)
    inner_act = jnp.dot(normed_mid, w_up, preferred_element_type=jnp.float32) + b_up
    active = jax.nn.gelu(inner_act, approximate=False).astype(jnp.bfloat16)
    ffn_out = lax.psum_scatter(
        jnp.dot(active, w_down, preferred_element_type=jnp.float32).astype(jnp.bfloat16),
        "head",
        scatter_dimension=1,
        tiled=True,
    ).astype(jnp.float32)
    down_bias_share = lax.dynamic_slice_in_dim(b_down, head_pos * slice_width, slice_width, 0)
    layer_output = (middle + (ffn_out + down_bias_share)).astype(jnp.bfloat16)
    grad_whole = lax.all_gather(cotangent, "head", axis=1, tiled=True)
    grad_float = grad_whole.astype(jnp.float32)
    grad_w_down = jnp.dot(active.T, grad_whole, preferred_element_type=jnp.float32)
    grad_b_down = jnp.sum(grad_float, axis=0)
    grad_active = jnp.dot(grad_whole, w_down.T, preferred_element_type=jnp.float32)
    unused, gelu_back = jax.vjp(lambda inputs: jax.nn.gelu(inputs, approximate=False), inner_act)
    grad_inner = gelu_back(grad_active)[0].astype(jnp.bfloat16)
    grad_w_up = jnp.dot(normed_mid.T, grad_inner, preferred_element_type=jnp.float32)
    grad_b_up = jnp.sum(grad_inner.astype(jnp.float32), axis=0)
    grad_norm_mid = lax.psum(
        jnp.dot(grad_inner, w_up.T, preferred_element_type=jnp.float32).astype(jnp.bfloat16), "head"
    ).astype(jnp.float32)
    unused, mid_back = jax.vjp(layer_norm, middle_whole, ln2_gain, ln2_bias)
    grad_mid_norm, grad_ln2_gain, grad_ln2_bias = mid_back(grad_norm_mid)
    grad_middle = grad_float + grad_mid_norm
    grad_branch = grad_middle.astype(jnp.bfloat16)
    grad_b_out = jnp.sum(grad_branch.astype(jnp.float32), axis=0)
    grad_w_out = jnp.dot(sub_out.T, grad_branch, preferred_element_type=jnp.float32)
    grad_sub = jnp.dot(grad_branch, w_out.T, preferred_element_type=jnp.float32)
    grad_sub_gain = jnp.sum(grad_sub * centered, axis=0)
    grad_sub_bias = jnp.sum(grad_sub, axis=0)
    grad_hat = grad_sub * sub_gain
    hat_sum, hat_cross = lax.psum(
        (jnp.sum(grad_hat, axis=1), jnp.sum(grad_hat * centered, axis=1)), "head"
    )
    grad_mixed = inv_std[:, None] * (
        grad_hat - hat_sum[:, None] / full_width - centered * hat_cross[:, None] / full_width
    )
    grad_heads = (
        grad_mixed.reshape(rows_local, local_heads, HEAD_DIM)
        .transpose(1, 0, 2)
        .astype(jnp.bfloat16)
    )
    dot_term = jnp.sum(grad_heads.astype(jnp.float32) * attended, axis=-1)
    key_all, value_all = (
        lax.all_gather(key_rows, "seq", axis=0, tiled=True),
        lax.all_gather(values, "seq", axis=0, tiled=True),
    )
    total_rows = key_all.shape[0]
    block_rows = math.gcd(total_rows, 2048)
    key_blocks = key_all.reshape(total_rows // block_rows, block_rows, local_heads, HEAD_DIM)
    value_blocks = value_all.reshape(total_rows // block_rows, block_rows, local_heads, HEAD_DIM)
    offsets = jnp.arange(total_rows // block_rows, dtype=jnp.int32) * block_rows

    def score_parts(
        query_blk, grad_blk, log_blk, dot_blk, q_row, q_place, key_blk, value_blk, k_row, k_place
    ):
        counted = pattern_count(head_ids, q_row, q_place, k_row, k_place)
        scores = (
            jnp.einsum("hqd,khd->hqk", query_blk, key_blk, preferred_element_type=jnp.float32)
            * score_scale
        )
        masked = jnp.where(counted > 0, scores, -1e30)
        weights_norm = counted * jnp.exp(masked - log_blk[..., None])
        grad_probs = jnp.einsum(
            "hqd,khd->hqk", grad_blk, value_blk, preferred_element_type=jnp.float32
        )
        grad_scores = (weights_norm * (grad_probs - dot_blk[..., None])).astype(jnp.bfloat16)
        return (weights_norm, grad_scores)

    def back_step(grad_query_sum, element):
        key_blk, value_blk, block_first = element
        key_row, key_place = token_places(
            block_first + jnp.arange(block_rows, dtype=jnp.int32), row_lengths
        )
        weights_norm, grad_scores = score_parts(
            query_heads,
            grad_heads,
            log_total,
            dot_term,
            query_row,
            query_place,
            key_blk,
            value_blk,
            key_row,
            key_place,
        )
        grad_query_sum = grad_query_sum + jnp.einsum(
            "hqk,khd->hqd", grad_scores, key_blk, preferred_element_type=jnp.float32
        )
        grad_value = jnp.einsum(
            "hqk,hqd->khd",
            weights_norm.astype(jnp.bfloat16),
            grad_heads,
            preferred_element_type=jnp.float32,
        )
        grad_key = jnp.einsum(
            "hqk,hqd->khd", grad_scores, query_heads, preferred_element_type=jnp.float32
        )
        key_terms = jnp.concatenate(
            [grad_key.reshape(block_rows, -1) * score_scale, grad_value.reshape(block_rows, -1)],
            axis=1,
        )
        return (grad_query_sum, key_terms)

    query_zero = jnp.zeros((local_heads, rows_local, HEAD_DIM), jnp.float32)
    grad_query_sum, key_terms = lax.scan(back_step, query_zero, (key_blocks, value_blocks, offsets))
    key_terms = key_terms.reshape(total_rows, 2 * head_share)
    kv_grads = lax.psum_scatter(key_terms, "seq", scatter_dimension=0, tiled=True)
    grad_keys = kv_grads[:, :head_share].astype(jnp.bfloat16)
    grad_values = kv_grads[:, head_share:].astype(jnp.bfloat16)
    grad_queries = (grad_query_sum * score_scale).transpose(1, 0, 2).reshape(rows_local, head_share)
    grad_queries = grad_queries.astype(jnp.bfloat16)
    grad_w_query = jnp.dot(normed.T, grad_queries, preferred_element_type=jnp.float32)
    grad_b_query = jnp.sum(grad_queries.astype(jnp.float32), axis=0)
    grad_w_key = jnp.dot(normed.T, grad_keys, preferred_element_type=jnp.float32)
    grad_w_value = jnp.dot(normed.T, grad_values, preferred_element_type=jnp.float32)
    grad_b_value = jnp.sum(grad_values.astype(jnp.float32), axis=0)
    grad_normed = (
        jnp.dot(grad_queries, w_query.T, preferred_element_type=jnp.float32)
        + jnp.dot(grad_keys, w_key.T, preferred_element_type=jnp.float32)
        + jnp.dot(grad_values, w_value.T, preferred_element_type=jnp.float32)
    )
    grad_normed = lax.psum(grad_normed.astype(jnp.bfloat16), "head").astype(jnp.float32)
    unused, input_back = jax.vjp(layer_norm, input_whole, ln1_gain, ln1_bias)
    grad_in_norm, grad_ln1_gain, grad_ln1_bias = input_back(grad_normed)
    grad_input_whole = grad_middle + grad_in_norm
    grad_input = lax.dynamic_slice_in_dim(grad_input_whole, head_pos * slice_width, slice_width, 1)
    summed = lax.psum(
        (
            grad_ln1_gain,
            grad_ln1_bias,
            grad_w_query,
            grad_b_query,
            grad_w_key,
            grad_w_value,
            grad_b_value,
            grad_sub_gain,
            grad_sub_bias,
            grad_w_out,
            grad_b_out,
            grad_ln2_gain,
            grad_ln2_bias,
            grad_w_up,
            grad_b_up,
            grad_w_down,
            grad_b_down,
        ),
        "seq",
    )
    return (layer_output, grad_input) + tuple(summed)


def solution(mesh):
    in_specs = (
        P("seq", "head"),
        P(),
        P(),
        P(None, "head"),
        P("head"),
        P(None, "head"),
        P(None, "head"),
        P("head"),
        P("head"),
        P("head"),
        P("head", None),
        P(),
        P(),
        P(),
        P(None, "head"),
        P("head"),
        P("head", None),
        P(),
        P("seq", "head"),
        P(),
    )
    out_specs = (
        P("seq", "head"),
        P("seq", "head"),
        P(),
        P(),
        P(None, "head"),
        P("head"),
        P(None, "head"),
        P(None, "head"),
        P("head"),
        P("head"),
        P("head"),
        P("head", None),
        P(),
        P(),
        P(),
        P(None, "head"),
        P("head"),
        P("head", None),
        P(),
    )
    return jax.shard_map(shards, mesh=mesh, in_specs=in_specs, out_specs=out_specs, check_vma=False)
```

profile of v0, /device:TPU:0, one launch (start us, length us, event | category | flops | bytes accessed | tf_op | source)
XLA Modules:
  0.0 842.8 jit_solution(17732856070422200237)
XLA Ops:
  7.3 10.4 %all_gather.17 = bf16[512,768]{0,1:T(8,128)(2,1)S(1)} all-gather(bf16[512,192]{0,1:T(8,128)(2,1)} %param.24), channel_id=1, replica_groups=mesh['seq'=8,'head'=4] {'head'}, dimensions={1}, use_global_device_ids=true | all-gather | bytes 983040 | tf_op jit(solution)/shard_map/all_gather | solution.py:121
  22.7 43.9 %all-gather.3.cloned.1.call-done = bf16[4096,192]{0,1:T(8,128)(2,1)} async-done(((bf16[512,192]{0,1:T(8,128)(2,1)}), bf16[4096,192]{0,1:T(8,128)(2,1)}) %all-gather.3.cloned.1.call-update) | async-done | bytes 1572880 | tf_op jit(solution)/shard_map/all_gather | solution.py:139
  66.6 2.9 reshape.2798
  69.5 1.8 copy.68
  71.2 41.5 %all-gather.5.cloned.1.call-done = bf16[4096,192]{0,1:T(8,128)(2,1)} async-done(((bf16[512,192]{0,1:T(8,128)(2,1)}), bf16[4096,192]{0,1:T(8,128)(2,1)}) %all-gather.5.cloned.1.call-update) | async-done | bytes 1572880 | tf_op jit(solution)/shard_map/all_gather | solution.py:140
  112.8 2.9 reshape.2800
  115.6 1.8 copy.69
  117.4 77.7 %while.42 = (s32[]{:T(128)}, f32[3,512]{1,0:T(4,128)S(1)}, f32[3,512]{1,0:T(4,128)}, f32[3,512,64]{1,2,0:T(8,128)}, s32[512]{0:T(512)S(1)}, /*index=5*/s32[2]{0:...) while((s32[]{:T(128)}, f32[3,512]{1,0:T(4,128)S(1)}, ...), condition=%wide.region_10.11_spmd.clone.clone.clone, body=%wide.region_5.10_spmd.clone.clone.clone.sunk | while | flops 955956864 | bytes 106965376 | solution.py:84
  120.3 4.1 compare_and_fusion.12
  125.2 12.1 %fusion.202 = (f32[3,512]{1,0:T(4,128)S(1)}, f32[3,2048,512]{2,1,0:T(8,128)}) fusion(f32[512,2048]{0,1:T(8,128)S(1)} %get-tuple-element.1711, pred[3,2048]{1,0:T(4,128)(4,1)S(1)} %broadcast_compare_fusion.38, pred[3,512]{1,0:T(4,128)(4,1)S(1)} %broadcast_compare_fusion.39, pred[512,2048]{0,1:T(8,128)(4,1)S(1)} %get-tuple-element.1716, ...), kind=kOutput, calls=%fused_computation.7.clone.1 | convolution fusion | flops 465566208 | bytes 22001668 | tf_op jit(solution)/shard_map/while/body/eval_jaxpr/hqd,khd->hqk/dot_general | solution.py:68
  137.4 16.7 %fusion.203 = (f32[3,512]{1,0:T(4,128)S(1)}, bf16[3,512,2048]{1,2,0:T(8,128)(2,1)S(1)}) fusion(f32[3,512]{1,0:T(4,128)S(1)} %select_maximum_fusion.2, f32[3,2048,512]{2,1,0:T(8,128)} %get-tuple-element.1730, pred[3,2048]{1,0:T(4,128)(4,1)S(1)} %broadcast_compare_fusion.38, pred[3,512]{1,0:T(4,128)(4,1)S(1)} %broadcast_compare_fusion.39, ...), kind=kLoop, calls=%fused_computation.388.clone.1 | loop fusion | flops 72350208 | bytes 27305984 | tf_op jit(solution)/shard_map/while/body/eval_jaxpr/reduce_sum | solution.py:75
  159.2 4.1 compare_and_fusion.12
  164.1 12.1 %fusion.202 = (f32[3,512]{1,0:T(4,128)S(1)}, f32[3,2048,512]{2,1,0:T(8,128)}) fusion(f32[512,2048]{0,1:T(8,128)S(1)} %get-tuple-element.1711, pred[3,2048]{1,0:T(4,128)(4,1)S(1)} %broadcast_compare_fusion.38, pred[3,512]{1,0:T(4,128)(4,1)S(1)} %broadcast_compare_fusion.39, pred[512,2048]{0,1:T(8,128)(4,1)S(1)} %get-tuple-element.1716, ...), kind=kOutput, calls=%fused_computation.7.clone.1 | convolution fusion | flops 465566208 | bytes 22001668 | tf_op jit(solution)/shard_map/while/body/eval_jaxpr/hqd,khd->hqk/dot_general | solution.py:68
  176.3 16.7 %fusion.203 = (f32[3,512]{1,0:T(4,128)S(1)}, bf16[3,512,2048]{1,2,0:T(8,128)(2,1)S(1)}) fusion(f32[3,512]{1,0:T(4,128)S(1)} %select_maximum_fusion.2, f32[3,2048,512]{2,1,0:T(8,128)} %get-tuple-element.1730, pred[3,2048]{1,0:T(4,128)(4,1)S(1)} %broadcast_compare_fusion.38, pred[3,512]{1,0:T(4,128)(4,1)S(1)} %broadcast_compare_fusion.39, ...), kind=kLoop, calls=%fused_computation.388.clone.1 | loop fusion | flops 72350208 | bytes 27305984 | tf_op jit(solution)/shard_map/while/body/eval_jaxpr/reduce_sum | solution.py:75
  196.4 6.0 all-reduce.3
  204.9 8.7 %all_gather.21 = bf16[512,768]{0,1:T(8,128)(2,1)S(1)} all-gather(bf16[512,192]{0,1:T(8,128)(2,1)} %param.42), channel_id=1, replica_groups=mesh['seq'=8,'head'=4] {'head'}, dimensions={1}, use_global_device_ids=true | all-gather | bytes 983040 | tf_op jit(solution)/shard_map/all_gather | solution.py:181
  213.6 11.9 %reduce-scatter.4.cloned.1.call-done = bf16[512,192]{0,1:T(8,128)(2,1)} async-done(((bf16[512,768]{0,1:T(8,128)(2,1)}), bf16[512,192]{0,1:T(8,128)(2,1)}) %reduce-scatter.4.cloned.1.call-update) | async-done | bytes 196624 | tf_op jit(solution)/shard_map/reduce_scatter | solution.py:159
  226.7 8.4 all_gather.20
  236.7 5.8 convert_reduce_fusion.7
  243.4 1.7 convolution_convert_fusion
  245.9 34.5 %all-reduce.8.cloned.1.call-done = bf16[512,768]{0,1:T(8,128)(2,1)} async-done(((bf16[512,768]{0,1:T(8,128)(2,1)}), bf16[512,768]{0,1:T(8,128)(2,1)}) %all-reduce.8.cloned.1.call-update) | async-done | bytes 786448 | tf_op jit(solution)/shard_map/psum | solution.py:190
  280.3 2.4 convert_reduce_fusion.3
  282.8 1.5 fusion.102
  284.3 1.6 convert_reduce_fusion.8
  287.2 1.6 multiply_reduce_fusion
  288.8 6.6 all-reduce.2
  297.7 104.5 %while.43 = (s32[]{:T(128)}, f32[3,512,64]{1,2,0:T(8,128)S(1)}, f32[2,2048,384]{2,1,0:T(8,128)}, s32[512]{0:T(512)S(1)}, s32[2]{0:T(128)}, /*index=5*/s32[6,1]{0...) while((s32[]{:T(128)}, f32[3,512,64]{1,2,0:T(8,128)S(1)}, ...), condition=%wide.region_30.31_spmd.clone.clone.clone, body=%wide.region_27.30_spmd.clone.clone.clone.sunk | while | flops 2108366976 | bytes 175255120 | solution.py:277
  303.9 4.1 compare_and_fusion.13
  308.7 12.4 %fusion.216 = f32[3,512,2048]{1,2,0:T(8,128)S(1)} fusion(f32[3,512]{1,0:T(4,128)S(1)} %copy-done.86, f32[512,2048]{0,1:T(8,128)S(1)} %get-tuple-element.1766, pred[3,2048]{1,0:T(4,128)(4,1)S(1)} %broadcast_compare_fusion.46, pred[3,512]{1,0:T(4,128)(4,1)S(1)} %broadcast_compare_fusion.47, pred[512,2048]{0,1:T(8,128)(4,1)S(1)} %get-tuple-element.1771, ...), kind=kOutput, calls=%fused_computation.139.clone.1 | convolution fusion | flops 468713472 | bytes 22003716 | tf_op jit(solution)/shard_map/while/body/eval_jaxpr/hqd,khd->hqk/dot_general | solution.py:230
  321.2 5.1 fusion.217
  327.6 4.4 convolution_add_fusion.5
  332.1 6.7 fusion.218
  338.8 2.0 convolution_multiply_fusion.2
  340.8 1.9 maximum_bitcast_fusion.2
  342.7 3.5 copy.112
  346.2 3.7 constant_dynamic-update-slice_fusion.2
  356.1 4.1 compare_and_fusion.13
  360.9 12.4 %fusion.216 = f32[3,512,2048]{1,2,0:T(8,128)S(1)} fusion(f32[3,512]{1,0:T(4,128)S(1)} %copy-done.86, f32[512,2048]{0,1:T(8,128)S(1)} %get-tuple-element.1766, pred[3,2048]{1,0:T(4,128)(4,1)S(1)} %broadcast_compare_fusion.46, pred[3,512]{1,0:T(4,128)(4,1)S(1)} %broadcast_compare_fusion.47, pred[512,2048]{0,1:T(8,128)(4,1)S(1)} %get-tuple-element.1771, ...), kind=kOutput, calls=%fused_computation.139.clone.1 | convolution fusion | flops 468713472 | bytes 22003716 | tf_op jit(solution)/shard_map/while/body/eval_jaxpr/hqd,khd->hqk/dot_general | solution.py:230
  373.4 5.1 fusion.217
  379.8 4.4 convolution_add_fusion.5
  384.3 6.7 fusion.218
  391.0 2.0 convolution_multiply_fusion.2
  393.0 1.9 maximum_bitcast_fusion.2
  394.9 3.5 copy.112
  398.5 3.8 constant_dynamic-update-slice_fusion.2
  402.5 2.1 multiply_convert_fusion
  404.6 1.7 convolution_convert_fusion.1
  406.4 2.2 fusion.144
  408.7 2.3 fusion.131
  413.3 2.5 fusion.142
  417.1 103.4 %reduce-scatter.8.cloned.1.call-done = f32[512,384]{1,0:T(8,128)} async-done(((f32[4096,384]{1,0:T(8,128)}), f32[512,384]{1,0:T(8,128)}) %reduce-scatter.8.cloned.1.call-update) | async-done | bytes 786448 | tf_op jit(solution)/shard_map/reduce_scatter | solution.py:279
  521.9 1.5 fusion.117
  524.9 2.3 fusion.115
  527.2 1.4 fusion.119
  531.3 14.2 %reduce-scatter.6.cloned.1.call-done = bf16[512,192]{0,1:T(8,128)(2,1)} async-done(((bf16[512,768]{0,1:T(8,128)(2,1)}), bf16[512,192]{0,1:T(8,128)(2,1)}) %reduce-scatter.6.cloned.1.call-update) | async-done | bytes 196624 | tf_op jit(solution)/shard_map/reduce_scatter | solution.py:173
  545.5 2.0 add_convert_fusion.2
  547.5 1.7 convert_reduce_fusion.9
  549.2 33.4 %all-reduce.10.cloned.1.call-done = bf16[512,768]{0,1:T(8,128)(2,1)} async-done(((bf16[512,768]{0,1:T(8,128)(2,1)}), bf16[512,768]{0,1:T(8,128)(2,1)}) %all-reduce.10.cloned.1.call-update) | async-done | bytes 786448 | tf_op jit(solution)/shard_map/psum | solution.py:294
  582.6 2.5 fusion.103
  585.1 40.1 %all-reduce = (f32[768]{0:T(1024)}, f32[768]{0:T(1024)}, f32[192]{0:T(256)}, f32[192]{0:T(256)}, f32[192]{0:T(256)}, /*index=5*/f32[192]{0:T(256)}, f32[768]{0:T...) all-reduce(f32[768]{0:T(1024)} %get-tuple-element.1251, ...), channel_id=1, replica_groups=mesh['seq'=8,'head'=4] {'seq'}, use_global_device_ids=true, to_apply=%region_36.37 | all-reduce | flops 6144 | bytes 49152 | tf_op jit(solution)/shard_map/psum | solution.py:299
  625.9 1.6 fusion.138
  628.4 198.8 %all-reduce.12.cloned.1.call-done = (f32[768,192]{0,1:T(8,128)}, f32[768,192]{0,1:T(8,128)}, f32[768,192]{0,1:T(8,128)}, f32[192,768]{1,0:T(8,128)}, f32[768,768]{1,0:T(8,128)}, /*index=5*/f32[768,768]{1,0:T(8,128)}) async-done(((f32[768,192]{0,1:T(8,128)}, f32[768,192]{0,1:T(8,128)}, f32[768,192]{0,1:T(8,128)}, f32[192,768]{1,0:T(8,128)}, f32[768,768]{1,0:T(8,128)}, /*index=5*/f32[768,768]{1,0:T(8,128)}), ...) | async-done | bytes 7077904 | tf_op jit(solution)/shard_map/psum | solution.py:299
  827.1 2.0 copy.143
  831.6 1.4 copy.147
  (413 shorter events, 59.7 us)
Async XLA Ops:
  7.2 229.5 %copy-start = (bf16[768,768]{1,0:T(8,128)(2,1)S(1)}, bf16[768,768]{1,0:T(8,128)(2,1)}, u32[]{:S(2)}) copy-start(bf16[768,768]{1,0:T(8,128)(2,1)} %param.40) | copy-start | bytes 3538948
  7.2 11.5 %copy-start.87 = (f32[768]{0:T(1024)S(1)}, f32[768]{0:T(1024)}, u32[]{:S(2)}) copy-start(f32[768]{0:T(1024)} %param.26) | copy-start | bytes 9220
  7.2 11.5 %copy-start.70 = (f32[768]{0:T(1024)S(1)}, f32[768]{0:T(1024)}, u32[]{:S(2)}) copy-start(f32[768]{0:T(1024)} %param.25) | copy-start | bytes 9220
  7.2 59.4 %all-gather.3.cloned.1.call-start = ((), (), s32[]{:S(2)}) async-start(), calls=%async_computation.3 | async-start | bytes 1769472 | tf_op jit(solution)/shard_map/all_gather | solution.py:139
  20.3 92.5 %all-gather.5.cloned.1.call-start = ((), (), s32[]{:S(2)}) async-start(), calls=%async_computation.4 | async-start | bytes 1769472 | tf_op jit(solution)/shard_map/all_gather | solution.py:140
  21.4 204.1 %reduce-scatter.4.cloned.1.call-start = ((), (), s32[]{:S(2)}) async-start(), calls=%async_computation.5 | async-start | bytes 983040 | tf_op jit(solution)/shard_map/reduce_scatter | solution.py:159
  124.5 12.8 %copy-start.2 = (f32[512,2048]{0,1:T(8,128)}, f32[512,2048]{0,1:T(8,128)S(1)}, u32[]{:S(2)}) copy-start(f32[512,2048]{0,1:T(8,128)S(1)} %get-tuple-element.1711) | copy-start | bytes 12582916 | tf_op jit(solution)/shard_map/while
  124.5 12.8 %copy-start.3 = (pred[512,2048]{0,1:T(8,128)(4,1)}, pred[512,2048]{0,1:T(8,128)(4,1)S(1)}, u32[]{:S(2)}) copy-start(pred[512,2048]{0,1:T(8,128)(4,1)S(1)} %get-tuple-element.1720) | copy-start | bytes 3145732 | tf_op jit(solution)/shard_map/while
  124.5 12.8 %copy-start.4 = (pred[512,2048]{0,1:T(8,128)(4,1)}, pred[512,2048]{0,1:T(8,128)(4,1)S(1)}, u32[]{:S(2)}) copy-start(pred[512,2048]{0,1:T(8,128)(4,1)S(1)} %get-tuple-element.1716) | copy-start | bytes 3145732 | tf_op jit(solution)/shard_map/while
  125.1 12.3 %copy-start.55 = (pred[3,512]{1,0:T(4,128)(4,1)}, pred[3,512]{1,0:T(4,128)(4,1)S(1)}, u32[]{:S(2)}) copy-start(pred[3,512]{1,0:T(4,128)(4,1)S(1)} %broadcast_compare_fusion.43) | copy-start | bytes 4612 | tf_op jit(solution)/shard_map/while
  125.2 12.1 %copy-start.56 = (pred[3,512]{1,0:T(4,128)(4,1)}, pred[3,512]{1,0:T(4,128)(4,1)S(1)}, u32[]{:S(2)}) copy-start(pred[3,512]{1,0:T(4,128)(4,1)S(1)} %broadcast_compare_fusion.45) | copy-start | bytes 4612 | tf_op jit(solution)/shard_map/while
  137.4 16.7 %copy-start.43 = (f32[3,512]{1,0:T(4,128)S(1)}, f32[3,512]{1,0:T(4,128)}, u32[]{:S(2)}) copy-start(f32[3,512]{1,0:T(4,128)} %get-tuple-element.1804) | copy-start | bytes 18436 | tf_op jit(solution)/shard_map/while
  137.4 16.8 %copy-start.5 = (bf16[2,2048,3,64]{1,3,2,0:T(8,128)(2,1)S(1)}, bf16[2,2048,3,64]{1,3,2,0:T(8,128)(2,1)}, u32[]{:S(2)}) copy-start(bf16[2,2048,3,64]{1,3,2,0:T(8,128)(2,1)} %get-tuple-element.1834) | copy-start | bytes 4718596 | tf_op jit(solution)/shard_map/while
  137.4 16.8 %copy-start.17 = (f32[3,512,64]{1,2,0:T(8,128)S(1)}, f32[3,512,64]{1,2,0:T(8,128)}, u32[]{:S(2)}) copy-start(f32[3,512,64]{1,2,0:T(8,128)} %get-tuple-element.1805) | copy-start | bytes 1179652 | tf_op jit(solution)/shard_map/while
  163.4 12.8 %copy-start.2 = (f32[512,2048]{0,1:T(8,128)}, f32[512,2048]{0,1:T(8,128)S(1)}, u32[]{:S(2)}) copy-start(f32[512,2048]{0,1:T(8,128)S(1)} %get-tuple-element.1711) | copy-start | bytes 12582916 | tf_op jit(solution)/shard_map/while
  163.4 12.8 %copy-start.3 = (pred[512,2048]{0,1:T(8,128)(4,1)}, pred[512,2048]{0,1:T(8,128)(4,1)S(1)}, u32[]{:S(2)}) copy-start(pred[512,2048]{0,1:T(8,128)(4,1)S(1)} %get-tuple-element.1720) | copy-start | bytes 3145732 | tf_op jit(solution)/shard_map/while
  163.4 12.8 %copy-start.4 = (pred[512,2048]{0,1:T(8,128)(4,1)}, pred[512,2048]{0,1:T(8,128)(4,1)S(1)}, u32[]{:S(2)}) copy-start(pred[512,2048]{0,1:T(8,128)(4,1)S(1)} %get-tuple-element.1716) | copy-start | bytes 3145732 | tf_op jit(solution)/shard_map/while
  163.9 12.3 %copy-start.55 = (pred[3,512]{1,0:T(4,128)(4,1)}, pred[3,512]{1,0:T(4,128)(4,1)S(1)}, u32[]{:S(2)}) copy-start(pred[3,512]{1,0:T(4,128)(4,1)S(1)} %broadcast_compare_fusion.43) | copy-start | bytes 4612 | tf_op jit(solution)/shard_map/while
  164.1 12.1 %copy-start.56 = (pred[3,512]{1,0:T(4,128)(4,1)}, pred[3,512]{1,0:T(4,128)(4,1)S(1)}, u32[]{:S(2)}) copy-start(pred[3,512]{1,0:T(4,128)(4,1)S(1)} %broadcast_compare_fusion.45) | copy-start | bytes 4612 | tf_op jit(solution)/shard_map/while
  176.3 16.7 %copy-start.43 = (f32[3,512]{1,0:T(4,128)S(1)}, f32[3,512]{1,0:T(4,128)}, u32[]{:S(2)}) copy-start(f32[3,512]{1,0:T(4,128)} %get-tuple-element.1804) | copy-start | bytes 18436 | tf_op jit(solution)/shard_map/while
  176.3 16.8 %copy-start.5 = (bf16[2,2048,3,64]{1,3,2,0:T(8,128)(2,1)S(1)}, bf16[2,2048,3,64]{1,3,2,0:T(8,128)(2,1)}, u32[]{:S(2)}) copy-start(bf16[2,2048,3,64]{1,3,2,0:T(8,128)(2,1)} %get-tuple-element.1834) | copy-start | bytes 4718596 | tf_op jit(solution)/shard_map/while
  176.3 16.8 %copy-start.17 = (f32[3,512,64]{1,2,0:T(8,128)S(1)}, f32[3,512,64]{1,2,0:T(8,128)}, u32[]{:S(2)}) copy-start(f32[3,512,64]{1,2,0:T(8,128)} %get-tuple-element.1805) | copy-start | bytes 1179652 | tf_op jit(solution)/shard_map/while
  195.1 7.3 copy-start.48
  195.1 7.3 copy-start.51
  195.2 7.3 copy-start.54
  195.2 8.8 %copy-start.59 = (s32[6,1]{0,1:T(1,128)}, s32[6,1]{0,1:T(1,128)S(1)}, u32[]{:S(2)}) copy-start(s32[6,1]{0,1:T(1,128)S(1)} %get-tuple-element.1979) | copy-start | bytes 76
  195.2 8.8 %copy-start.62 = (s32[1,6]{1,0:T(1,128)}, s32[1,6]{1,0:T(1,128)S(1)}, u32[]{:S(2)}) copy-start(s32[1,6]{1,0:T(1,128)S(1)} %get-tuple-element.1980) | copy-start | bytes 76
  195.2 7.4 copy-start.37
  195.2 7.4 copy-start.82
  195.2 7.4 copy-start.88
  196.3 7.7 copy-start.19
  202.5 11.1 %copy-start.76 = (f32[512]{0:T(512)}, f32[512]{0:T(512)S(1)}, u32[]{:S(2)}) copy-start(f32[512]{0:T(512)S(1)} %get-tuple-element.1435) | copy-start | bytes 6148
  202.5 11.1 %copy-start.78 = (f32[512]{0:T(512)}, f32[512]{0:T(512)S(1)}, u32[]{:S(2)}) copy-start(f32[512]{0:T(512)S(1)} %get-tuple-element.1436) | copy-start | bytes 6148
  202.6 10.9 %copy-start.27 = (f32[512,192]{0,1:T(8,128)}, f32[512,192]{0,1:T(8,128)S(1)}, u32[]{:S(2)}) copy-start(f32[512,192]{0,1:T(8,128)S(1)} %fusion.112) | copy-start | bytes 1179652
  202.6 22.9 %copy-start.32 = (bf16[512,192]{0,1:T(8,128)(2,1)S(1)}, bf16[512,192]{0,1:T(8,128)(2,1)}, u32[]{:S(2)}) copy-start(bf16[512,192]{0,1:T(8,128)(2,1)} %param.24) | copy-start | bytes 589828
  204.0 76.3 %all-reduce.8.cloned.1.call-start = ((), (), s32[]{:S(2)}) async-start(), calls=%async_computation.7 | async-start | bytes 1572864 | tf_op jit(solution)/shard_map/psum | solution.py:190
  204.9 30.3 %copy-start.85 = (f32[192]{0:T(256)}, f32[192]{0:T(256)S(1)}, u32[]{:S(2)}) copy-start(f32[192]{0:T(256)S(1)} %dynamic_slice.65) | copy-start | bytes 2308
  213.5 23.1 %copy-start.23 = (bf16[512,768]{0,1:T(8,128)(2,1)}, bf16[512,768]{0,1:T(8,128)(2,1)S(1)}, u32[]{:S(2)}) copy-start(bf16[512,768]{0,1:T(8,128)(2,1)S(1)} %all_gather.21) | copy-start | bytes 2359300
  213.5 21.9 %copy-start.67 = (f32[768]{0:T(1024)S(1)}, f32[768]{0:T(1024)}, u32[]{:S(2)}) copy-start(f32[768]{0:T(1024)} %param.36) | copy-start | bytes 9220
  213.6 21.9 %copy-start.93 = (f32[768]{0:T(1024)S(1)}, f32[768]{0:T(1024)}, u32[]{:S(2)}) copy-start(f32[768]{0:T(1024)} %param.39) | copy-start | bytes 9220
  213.6 21.9 %copy-start.94 = (f32[768]{0:T(1024)S(1)}, f32[768]{0:T(1024)}, u32[]{:S(2)}) copy-start(f32[768]{0:T(1024)} %param.37) | copy-start | bytes 9220
  225.5 10.0 %copy-start.92 = (bf16[768,768]{1,0:T(8,128)(2,1)S(1)}, bf16[768,768]{1,0:T(8,128)(2,1)}, u32[]{:S(2)}) copy-start(bf16[768,768]{1,0:T(8,128)(2,1)} %param.38) | copy-start | bytes 3538948
  235.0 49.3 %copy-start.9 = (bf16[512,768]{0,1:T(8,128)(2,1)}, bf16[512,768]{0,1:T(8,128)(2,1)S(1)}, u32[]{:S(2)}) copy-start(bf16[512,768]{0,1:T(8,128)(2,1)S(1)} %all_gather.20) | copy-start | bytes 2359300
  235.2 49.1 %copy-start.65 = (f32[512]{0:T(512)}, f32[512]{0:T(512)S(1)}, u32[]{:S(2)}) copy-start(f32[512]{0:T(512)S(1)} %broadcast_multiply_fusion.1) | copy-start | bytes 6148
  235.5 48.8 %copy-start.74 = (f32[512]{0:T(512)}, f32[512]{0:T(512)S(1)}, u32[]{:S(2)}) copy-start(f32[512]{0:T(512)S(1)} %fusion.123) | copy-start | bytes 6148
  243.4 36.9 %copy-start.68 = (f32[768]{0:T(1024)S(1)}, f32[768]{0:T(1024)}, u32[]{:S(2)}) copy-start(f32[768]{0:T(1024)} %param.36) | copy-start | bytes 9220
  245.2 275.4 %reduce-scatter.8.cloned.1.call-start = ((), (), s32[]{:S(2)}) async-start(), calls=%async_computation.8 | async-start | bytes 7077888 | tf_op jit(solution)/shard_map/reduce_scatter | solution.py:279
  286.0 9.4 %copy-start.77 = (f32[512]{0:T(512)S(1)}, f32[512]{0:T(512)}, u32[]{:S(2)}) copy-start(f32[512]{0:T(512)} %copy-done.76) | copy-start | bytes 6148
  286.0 9.4 %copy-start.79 = (f32[512]{0:T(512)S(1)}, f32[512]{0:T(512)}, u32[]{:S(2)}) copy-start(f32[512]{0:T(512)} %copy-done.78) | copy-start | bytes 6148
  287.2 10.6 %copy-start.6 = (bf16[2,2048,3,64]{1,3,2,0:T(8,128)(2,1)S(1)}, bf16[2,2048,3,64]{1,3,2,0:T(8,128)(2,1)}, u32[]{:S(2)}) copy-start(bf16[2,2048,3,64]{1,3,2,0:T(8,128)(2,1)} %get-tuple-element.1936) | copy-start | bytes 4718596
  321.2 6.4 copy-start.1
  327.6 11.2 %slice-start = ((s8[6291456]{0:T(1024)(128)(4,1)}), s8[4194304]{0:T(1024)(128)(4,1)S(1)}, s32[]{:S(2)}) async-start(s8[6291456]{0:T(1024)(128)(4,1)} %bitcast.169), calls=%async_computation.11 | async-start | bytes 8388608 | tf_op jit(solution)/shard_map/while
  332.0 6.8 slice-start.1
  373.4 6.4 copy-start.1
  379.8 11.2 %slice-start = ((s8[6291456]{0:T(1024)(128)(4,1)}), s8[4194304]{0:T(1024)(128)(4,1)S(1)}, s32[]{:S(2)}) async-start(s8[6291456]{0:T(1024)(128)(4,1)} %bitcast.169), calls=%async_computation.11 | async-start | bytes 8388608 | tf_op jit(solution)/shard_map/while
  384.2 6.8 slice-start.1
  402.2 143.3 %reduce-scatter.6.cloned.1.call-start = ((), (), s32[]{:S(2)}) async-start(), calls=%async_computation.6 | async-start | bytes 983040 | tf_op jit(solution)/shard_map/reduce_scatter | solution.py:173
  411.0 171.6 %all-reduce.10.cloned.1.call-start = ((), (), s32[]{:S(2)}) async-start(), calls=%async_computation.9 | async-start | bytes 1572864 | tf_op jit(solution)/shard_map/psum | solution.py:294
  524.8 302.3 %all-reduce.12.cloned.1.call-start = ((), (), s32[]{:S(2)}) async-start(), calls=%async_computation.10 | async-start | bytes 14155776 | tf_op jit(solution)/shard_map/psum | solution.py:299
  528.6 54.0 %copy-start.64 = (f32[512]{0:T(512)S(1)}, f32[512]{0:T(512)}, u32[]{:S(2)}) copy-start(f32[512]{0:T(512)} %copy-done.63) | copy-start | bytes 6148
  528.6 54.0 %copy-start.71 = (f32[768]{0:T(1024)S(1)}, f32[768]{0:T(1024)}, u32[]{:S(2)}) copy-start(f32[768]{0:T(1024)} %param.25) | copy-start | bytes 9220
  528.6 54.0 %copy-start.73 = (f32[512]{0:T(512)S(1)}, f32[512]{0:T(512)}, u32[]{:S(2)}) copy-start(f32[512]{0:T(512)} %copy-done.72) | copy-start | bytes 6148
  528.6 54.0 %copy-start.12 = (bf16[512,768]{0,1:T(8,128)(2,1)S(1)}, bf16[512,768]{0,1:T(8,128)(2,1)}, u32[]{:S(2)}) copy-start(bf16[512,768]{0,1:T(8,128)(2,1)} %copy-done.11) | copy-start | bytes 2359300
  528.6 96.6 %copy-start.81 = (f32[512]{0:T(512)S(1)}, f32[512]{0:T(512)}, u32[]{:S(2)}) copy-start(f32[512]{0:T(512)} %copy-done.80) | copy-start | bytes 6148
  (71 other events, 182.2 us)
Sparse Core Ops, SparseCore 0:
  20.4 46.1 all-gather.2
  69.2 43.4 all-gather.4
  204.1 21.3 reduce-scatter.3
  245.3 34.9 all-reduce.7
  402.4 118.1 reduce-scatter.7
  523.1 22.3 reduce-scatter.5
  547.9 34.6 all-reduce.9
  589.3 237.7 all-reduce.11
where the time goes:
time: 852 us; the launch traced here: 843 us
  waiting for transfers between devices  482 us (57%)
  matrix products  120 us (14%)
  other arithmetic  95.7 us (11%)
  blocking collectives  80.1 us (9%)
  local copies, waits for them, and re-layouts  48.5 us (6%)
  between operations  15.4 us (2%)
    psum x1, waiting for transfers between devices, shards(): lax.psum((grad_ln1_gain, grad_ln1_bias, grad_w_query, grad_b_query, grad_...  199 us
    reduce_scatter x1, waiting for transfers between devices, shards(): lax.psum_scatter(key_terms, 'seq', scatter_dimension=0, tiled=True)  103 us
    all_gather x1, waiting for transfers between devices, shards(): lax.all_gather(key_rows, 'seq', axis=0, tiled=True)  43.9 us
    all_gather x1, waiting for transfers between devices, shards(): lax.all_gather(values, 'seq', axis=0, tiled=True)  41.5 us
    psum x1, blocking collectives, shards(): lax.psum((grad_ln1_gain, grad_ln1_bias, grad_w_query, grad_b_query, grad_...  40.1 us
    psum x1, waiting for transfers between devices, shards(): lax.psum(jnp.dot(grad_inner, w_up.T, preferred_element_type=jnp.float32)....  34.5 us
    psum x1, waiting for transfers between devices, shards(): lax.psum(grad_normed.astype(jnp.bfloat16), 'head').astype(jnp.float32)  33.4 us
    reduce_sum x2, other arithmetic, advance(): totals = totals * factor + jnp.sum(weights, axis=-1)  33.3 us
  transfers between devices with their start and end apart: 8, of which 8 were waited for; matrix products, arithmetic and copies ran while one was open for 5% of the time, Pallas kernels for 0%

commit v1 on v0

v1 whole, which is shorter than its diff:
```python
import functools
import math

import jax
import jax.numpy as jnp
import numpy as np
from jax import lax
from jax.experimental import pallas as pl
from jax.experimental.pallas import tpu as pltpu
from jax.sharding import PartitionSpec as P

HEAD_DIM = 64
SEG = 2048


eps = 1e-05
segment_scales = (1, 2, 4, 8, 16)
dilation_steps = (1, 2, 4, 6, 12)


def layer_norm(inputs, norm_gain, norm_bias):
    center = inputs - jnp.mean(inputs, axis=-1, keepdims=True)
    spread = jnp.mean(center * center, axis=-1, keepdims=True)
    return center * lax.rsqrt(spread + eps) * norm_gain + norm_bias


bf=jnp.bfloat16; f32=jnp.float32
scales=(1,2,4,8,16); steps=(1,2,4,6,12)
NT=(((1,),(1,)),((),()))
NN=(((1,),(0,)),((),()))
def dot(a,b,dims=NN): return lax.dot_general(a,b,dims,preferred_element_type=f32)

def features(total, lengths, head_ids, nh):
    nrow=lengths.shape[0]
    pos=jnp.arange(total,dtype=jnp.int32)
    tri=np.tril(np.ones((nrow,nrow),np.int32))
    ends=jnp.sum(tri*lengths[None,:],axis=1); starts=ends-lengths
    past=(pos[:,None]>=ends[None,:])
    row_start=jnp.sum(jnp.where(past,lengths[None,:],0),axis=1)
    place=pos-row_start
    sizes=[nrow+total//(SEG*s) for s in scales]
    nf=sum(sizes); width=-(-nh*nf//128)*128
    lane=np.arange(width); lh=lane//nf; lf=lane%nf
    jl=jnp.sum(jnp.where(lh[None,:]==np.arange(nh)[:,None],head_ids[:,None],0),axis=0)
    out=jnp.zeros((total,width),jnp.bool_); off=0
    for s,r,n in zip(scales,steps,sizes):
        w=SEG*s
        nseg=(lengths+(w-1))//w
        base=jnp.sum(jnp.where(past,nseg[None,:],0),axis=1)
        sg=base+place//w+off
        pm=place%w%r
        lanek=(lf>=off)&(lf<off+n)&(lh<nh)
        fl=jnp.where(lanek,lf,-1); jm=jnp.where(lanek,jl%r,-1)
        out=out|((sg[:,None]==fl[None,:])&(pm[:,None]==jm[None,:]))
        off+=n
    return out.astype(bf), nf

def head_pad(x,h,hi):
    part=x[:,64*h:64*h+64]; z=jnp.zeros_like(part)
    return jnp.concatenate([z,part] if hi else [part,z],axis=1)

def tile_needed(sc,i,n,bk):
    gb=sc[i]; own=sc[n]; st=sc[n+1]
    return gb, own, (gb<=own)&((gb+1)*bk>st)

def count_tile(fk,fq,h,nf,gb,own,bk,tq):
    lane=lax.broadcasted_iota(jnp.int32,fq.shape,1)
    fqh=jnp.where((lane>=h*nf)&(lane<(h+1)*nf),fq.astype(f32),0.0).astype(bf)
    c=dot(fk,fqh,NT)
    ks=gb*bk+lax.broadcasted_iota(jnp.int32,(bk,1),0); qs=own*tq+lax.broadcasted_iota(jnp.int32,(1,tq),1)
    return jnp.where(ks<=qs,c,0.0)

def fwd_kernel(nh,nf,n,sc,q,fq,kv,fk,out,lse,acc,m,l):
    i=pl.program_id(0); bk=kv.shape[1]; tq=q.shape[0]
    @pl.when(i==0)
    def _():
        acc[...]=jnp.zeros_like(acc); m[...]=jnp.full_like(m,-1e30); l[...]=jnp.zeros_like(l)
    gb,own,need=tile_needed(sc,i,n,bk)
    @pl.when(need)
    def _():
        kvT=kv[0].astype(f32).T.astype(bf)
        qs=(q[...].astype(f32)*0.125).astype(bf)
        for h in range(nh):
            kvh=kv[0,:,128*h:128*h+128]
            s=dot(kvh,head_pad(qs,h,0),NT)
            c=count_tile(fk[...],fq[...],h,nf,gb,own,bk,tq)
            s=jnp.where(c>0,s,-1e30)
            mo=m[h:h+1,:]; mn=jnp.maximum(mo,jnp.max(s,axis=0,keepdims=True))
            p=c*jnp.exp(s-mn)
            al=jnp.exp(mo-mn)
            l[h:h+1,:]=l[h:h+1,:]*al+jnp.sum(p,axis=0,keepdims=True)
            o=dot(kvT[128*h:128*h+128],p.astype(bf))
            acc[64*h:64*h+64,:]=acc[64*h:64*h+64,:]*al+o[64:,:]
            m[h:h+1,:]=mn
    @pl.when(i==n-1)
    def _():
        for h in range(nh):
            acc[64*h:64*h+64,:]=acc[64*h:64*h+64,:]/l[h:h+1,:]
        out[...]=acc[...].T
        lse[...]=m[...]+jnp.log(jnp.maximum(l[...],1e-30))

def bwd_kernel(nh,nf,n,sc,q,fq,do,att,lse,kv,fk,dq,dkv,dqT,dterm):
    i=pl.program_id(0); bk=kv.shape[1]; tq=q.shape[0]
    @pl.when(i==0)
    def _():
        dqT[...]=jnp.zeros_like(dqT)
        prod=do[...].astype(f32)*att[...]
        r=lax.broadcasted_iota(jnp.int32,(8,prod.shape[1]),0); c=lax.broadcasted_iota(jnp.int32,(8,prod.shape[1]),1)
        sel=jnp.where(c//64==r,1.0,0.0).astype(f32)
        dterm[...]=lax.dot_general(sel,prod,NT,precision=lax.Precision.HIGHEST,preferred_element_type=f32)
    gb,own,need=tile_needed(sc,i,n,bk)
    @pl.when(jnp.logical_not(need))
    def _(): dkv[...]=jnp.zeros_like(dkv)
    @pl.when(need)
    def _():
        kvT=kv[0].astype(f32).T.astype(bf)
        qs=(q[...].astype(f32)*0.125).astype(bf)
        for h in range(nh):
            kvh=kv[0,:,128*h:128*h+128]
            qh=head_pad(qs,h,0); doh=head_pad(do[...],h,1)
            s=dot(kvh,qh,NT)
            c=count_tile(fk[...],fq[...],h,nf,gb,own,bk,tq)
            p=c*jnp.exp(jnp.minimum(s-lse[h:h+1,:],1.0))
            ds=p*(dot(kvh,doh,NT)-dterm[h:h+1,:])
            pb=p.astype(bf); dsb=ds.astype(bf)
            dkv[0,:,128*h:128*h+128]=(dot(dsb,qh)+dot(pb,doh)).astype(dkv.dtype)
            o=dot(kvT[128*h:128*h+128],dsb)
            dqT[64*h:64*h+64,:]+=o[:64,:]
    @pl.when(i==n-1)
    def _(): dq[...]=(dqT[...].T*0.125).astype(dq.dtype)

def attend_fwd(q,F,nf,own,kv,sc,n):
    tq,wd=q.shape; nh=wd//64; bk=kv.shape[1]; W=F.shape[1]
    full=lambda a,b: pl.BlockSpec((a,b),lambda i,s:(0,0))
    gs=pltpu.PrefetchScalarGridSpec(num_scalar_prefetch=1,grid=(n,),
      in_specs=[full(tq,wd),pl.BlockSpec((tq,W),lambda i,s:(s[n],0)),pl.BlockSpec((1,bk,2*wd),lambda i,s:(i,0,0)),pl.BlockSpec((bk,W),lambda i,s:(s[i],0))],
      out_specs=[full(tq,wd),full(8,tq)],
      scratch_shapes=[pltpu.VMEM((wd,tq),f32),pltpu.VMEM((8,tq),f32),pltpu.VMEM((8,tq),f32)])
    return pl.pallas_call(functools.partial(fwd_kernel,nh,nf,n),grid_spec=gs,
      out_shape=[jax.ShapeDtypeStruct((tq,wd),f32),jax.ShapeDtypeStruct((8,tq),f32)],
      compiler_params=pltpu.CompilerParams(dimension_semantics=("arbitrary",),vmem_limit_bytes=48<<20),name="attend_fwd")(sc,q,F,kv,F)

def attend_bwd(q,F,nf,do,att,lse,kv,sc,n):
    tq,wd=q.shape; nh=wd//64; bk=kv.shape[1]; W=F.shape[1]
    full=lambda a,b: pl.BlockSpec((a,b),lambda i,s:(0,0))
    gs=pltpu.PrefetchScalarGridSpec(num_scalar_prefetch=1,grid=(n,),
      in_specs=[full(tq,wd),pl.BlockSpec((tq,W),lambda i,s:(s[n],0)),full(tq,wd),full(tq,wd),full(8,tq),pl.BlockSpec((1,bk,2*wd),lambda i,s:(i,0,0)),pl.BlockSpec((bk,W),lambda i,s:(s[i],0))],
      out_specs=[full(tq,wd),pl.BlockSpec((1,bk,2*wd),lambda i,s:(i,0,0))],
      scratch_shapes=[pltpu.VMEM((wd,tq),f32),pltpu.VMEM((8,tq),f32)])
    return pl.pallas_call(functools.partial(bwd_kernel,nh,nf,n),grid_spec=gs,
      out_shape=[jax.ShapeDtypeStruct((tq,wd),bf),jax.ShapeDtypeStruct(kv.shape,bf)],
      compiler_params=pltpu.CompilerParams(dimension_semantics=("arbitrary",),vmem_limit_bytes=48<<20),name="attend_bwd")(sc,q,F,do,att,lse,kv,F)

RING=(0,2,4,6,7,5,3,1)
FWD=[(RING[i],RING[(i+1)%8]) for i in range(8)]
BWD=[(b,a) for a,b in FWD]

def ring_gather(x):
    a=b=x; got=[x]; h=x.shape[0]//2
    for _ in range(3):
        a=lax.ppermute(a,"seq",FWD); b=lax.ppermute(b,"seq",BWD); got+=[a,b]
    got.append(jnp.concatenate([lax.ppermute(a[:h],"seq",FWD),lax.ppermute(b[h:],"seq",BWD)],axis=0))
    return got

def ring_order(seq_pos):
    ring=jnp.asarray(RING,jnp.int32)
    pos=jnp.sum(jnp.where(ring==seq_pos,jnp.arange(8,dtype=jnp.int32),0))
    return ring[(pos+jnp.asarray([0,-1,1,-2,2,-3,3,4],jnp.int32))%8]

def ring_scatter(t):
    add=lambda u,v:(u.astype(jnp.float32)+v.astype(jnp.float32)).astype(u.dtype)
    h=t[0].shape[0]//2
    a=lax.ppermute(t[7][:h],"seq",FWD); b=lax.ppermute(t[7][h:],"seq",BWD)
    a=jnp.concatenate([add(t[6][:h],a),t[6][h:]],axis=0); b=jnp.concatenate([t[5][:h],add(t[5][h:],b)],axis=0)
    a=lax.ppermute(a,"seq",FWD); b=lax.ppermute(b,"seq",BWD)
    a=add(t[4],a); b=add(t[3],b)
    a=lax.ppermute(a,"seq",FWD); b=lax.ppermute(b,"seq",BWD)
    a=add(t[2],a); b=add(t[1],b)
    a=lax.ppermute(a,"seq",FWD); b=lax.ppermute(b,"seq",BWD)
    return t[0].astype(jnp.float32)+a.astype(jnp.float32)+b.astype(jnp.float32)

def shards(
    layer_input,
    ln1_gain,
    ln1_bias,
    w_query,
    b_query,
    w_key,
    w_value,
    b_value,
    sub_gain,
    sub_bias,
    w_out,
    b_out,
    ln2_gain,
    ln2_bias,
    w_up,
    b_up,
    w_down,
    b_down,
    cotangent,
    row_lengths,
):
    rows_local = layer_input.shape[0]
    slice_width = layer_input.shape[1]
    head_share = w_query.shape[1]
    local_heads = head_share // HEAD_DIM
    head_pos = lax.axis_index("head")
    seq_pos = lax.axis_index("seq")
    full_width = head_share * lax.axis_size("head")
    head_ids = head_pos * local_heads + jnp.arange(local_heads, dtype=jnp.int32)
    input_whole = lax.all_gather(layer_input, "head", axis=1, tiled=True).astype(jnp.float32)
    normed = layer_norm(input_whole, ln1_gain, ln1_bias).astype(jnp.bfloat16)
    queries = (jnp.dot(normed, w_query, preferred_element_type=jnp.float32) + b_query).astype(
        jnp.bfloat16
    )
    key_rows = jnp.dot(normed, w_key, preferred_element_type=jnp.float32).astype(jnp.bfloat16)
    values = (jnp.dot(normed, w_value, preferred_element_type=jnp.float32) + b_value).astype(
        jnp.bfloat16
    )
    total=rows_local*lax.axis_size("seq")
    F,nf=features(total,row_lengths,head_ids,local_heads)
    first=seq_pos*rows_local
    run_ends=jnp.sum(np.tril(np.ones((row_lengths.shape[0],)*2,np.int32))*row_lengths[None,:],axis=1)
    row_begin=jnp.sum(jnp.where(first>=run_ends,row_lengths,0))
    kv=jnp.stack([key_rows.reshape(rows_local,local_heads,HEAD_DIM),values.reshape(rows_local,local_heads,HEAD_DIM)],axis=2).reshape(rows_local,2*head_share)
    n_seq=lax.axis_size("seq")
    if n_seq==8:
        kv_tiles=jnp.stack(ring_gather(kv),axis=0); order=ring_order(seq_pos)
    else:
        kv_tiles=lax.all_gather(kv,"seq",axis=0); order=jnp.arange(n_seq,dtype=jnp.int32)
    sc=jnp.concatenate([order,jnp.stack([seq_pos,row_begin]).astype(jnp.int32)])
    mixed_heads,lse=attend_fwd(queries,F,nf,None,kv_tiles,sc,n_seq)
    row_sum, row_square = lax.psum(
        (jnp.sum(mixed_heads, axis=1), jnp.sum(mixed_heads * mixed_heads, axis=1)), "head"
    )
    mean_value = row_sum / full_width
    inv_std = lax.rsqrt(row_square / full_width - mean_value * mean_value + eps)
    centered = (mixed_heads - mean_value[:, None]) * inv_std[:, None]
    sub_out = (centered * sub_gain + sub_bias).astype(jnp.bfloat16)
    projected = lax.psum_scatter(
        jnp.dot(sub_out, w_out, preferred_element_type=jnp.float32).astype(jnp.bfloat16),
        "head",
        scatter_dimension=1,
        tiled=True,
    ).astype(jnp.float32)
    out_bias_share = lax.dynamic_slice_in_dim(b_out, head_pos * slice_width, slice_width, 0)
    middle = layer_input.astype(jnp.float32) + (projected + out_bias_share)
    middle_whole = lax.all_gather(middle.astype(jnp.bfloat16), "head", axis=1, tiled=True).astype(
        middle.dtype
    )
    normed_mid = layer_norm(middle_whole, ln2_gain, ln2_bias).astype(jnp.bfloat16)
    inner_act = jnp.dot(normed_mid, w_up, preferred_element_type=jnp.float32) + b_up
    active = jax.nn.gelu(inner_act, approximate=False).astype(jnp.bfloat16)
    ffn_out = lax.psum_scatter(
        jnp.dot(active, w_down, preferred_element_type=jnp.float32).astype(jnp.bfloat16),
        "head",
        scatter_dimension=1,
        tiled=True,
    ).astype(jnp.float32)
    down_bias_share = lax.dynamic_slice_in_dim(b_down, head_pos * slice_width, slice_width, 0)
    layer_output = (middle + (ffn_out + down_bias_share)).astype(jnp.bfloat16)
    grad_whole = lax.all_gather(cotangent, "head", axis=1, tiled=True)
    grad_float = grad_whole.astype(jnp.float32)
    grad_w_down = jnp.dot(active.T, grad_whole, preferred_element_type=jnp.float32)
    grad_b_down = jnp.sum(grad_float, axis=0)
    grad_active = jnp.dot(grad_whole, w_down.T, preferred_element_type=jnp.float32)
    unused, gelu_back = jax.vjp(lambda inputs: jax.nn.gelu(inputs, approximate=False), inner_act)
    grad_inner = gelu_back(grad_active)[0].astype(jnp.bfloat16)
    grad_w_up = jnp.dot(normed_mid.T, grad_inner, preferred_element_type=jnp.float32)
    grad_b_up = jnp.sum(grad_inner.astype(jnp.float32), axis=0)
    grad_norm_mid = lax.psum(
        jnp.dot(grad_inner, w_up.T, preferred_element_type=jnp.float32).astype(jnp.bfloat16), "head"
    ).astype(jnp.float32)
    unused, mid_back = jax.vjp(layer_norm, middle_whole, ln2_gain, ln2_bias)
    grad_mid_norm, grad_ln2_gain, grad_ln2_bias = mid_back(grad_norm_mid)
    grad_middle = grad_float + grad_mid_norm
    grad_branch = grad_middle.astype(jnp.bfloat16)
    grad_b_out = jnp.sum(grad_branch.astype(jnp.float32), axis=0)
    grad_w_out = jnp.dot(sub_out.T, grad_branch, preferred_element_type=jnp.float32)
    grad_sub = jnp.dot(grad_branch, w_out.T, preferred_element_type=jnp.float32)
    grad_sub_gain = jnp.sum(grad_sub * centered, axis=0)
    grad_sub_bias = jnp.sum(grad_sub, axis=0)
    grad_hat = grad_sub * sub_gain
    hat_sum, hat_cross = lax.psum(
        (jnp.sum(grad_hat, axis=1), jnp.sum(grad_hat * centered, axis=1)), "head"
    )
    grad_mixed = inv_std[:, None] * (
        grad_hat - hat_sum[:, None] / full_width - centered * hat_cross[:, None] / full_width
    )
    grad_queries,dkv=attend_bwd(queries,F,nf,grad_mixed.astype(jnp.bfloat16),mixed_heads,lse,kv_tiles,sc,n_seq)
    if n_seq==8:
        kv_grads=ring_scatter([dkv[i] for i in range(8)])
    else:
        kv_grads=lax.psum_scatter(dkv,"seq",scatter_dimension=0,tiled=False).astype(jnp.float32)
    kv_grads=kv_grads.reshape(rows_local,local_heads,2,HEAD_DIM)
    grad_keys=kv_grads[:,:,0].reshape(rows_local,head_share).astype(jnp.bfloat16)
    grad_values=kv_grads[:,:,1].reshape(rows_local,head_share).astype(jnp.bfloat16)
    grad_w_query = jnp.dot(normed.T, grad_queries, preferred_element_type=jnp.float32)
    grad_b_query = jnp.sum(grad_queries.astype(jnp.float32), axis=0)
    grad_w_key = jnp.dot(normed.T, grad_keys, preferred_element_type=jnp.float32)
    grad_w_value = jnp.dot(normed.T, grad_values, preferred_element_type=jnp.float32)
    grad_b_value = jnp.sum(grad_values.astype(jnp.float32), axis=0)
    grad_normed = (
        jnp.dot(grad_queries, w_query.T, preferred_element_type=jnp.float32)
        + jnp.dot(grad_keys, w_key.T, preferred_element_type=jnp.float32)
        + jnp.dot(grad_values, w_value.T, preferred_element_type=jnp.float32)
    )
    grad_normed = lax.psum(grad_normed.astype(jnp.bfloat16), "head").astype(jnp.float32)
    unused, input_back = jax.vjp(layer_norm, input_whole, ln1_gain, ln1_bias)
    grad_in_norm, grad_ln1_gain, grad_ln1_bias = input_back(grad_normed)
    grad_input_whole = grad_middle + grad_in_norm
    grad_input = lax.dynamic_slice_in_dim(grad_input_whole, head_pos * slice_width, slice_width, 1)
    summed = lax.psum(
        (
            grad_ln1_gain,
            grad_ln1_bias,
            grad_w_query,
            grad_b_query,
            grad_w_key,
            grad_w_value,
            grad_b_value,
            grad_sub_gain,
            grad_sub_bias,
            grad_w_out,
            grad_b_out,
            grad_ln2_gain,
            grad_ln2_bias,
            grad_w_up,
            grad_b_up,
            grad_w_down,
            grad_b_down,
        ),
        "seq",
    )
    return (layer_output, grad_input) + tuple(summed)


def solution(mesh):
    in_specs = (
        P("seq", "head"),
        P(),
        P(),
        P(None, "head"),
        P("head"),
        P(None, "head"),
        P(None, "head"),
        P("head"),
        P("head"),
        P("head"),
        P("head", None),
        P(),
        P(),
        P(),
        P(None, "head"),
        P("head"),
        P("head", None),
        P(),
        P("seq", "head"),
        P(),
    )
    out_specs = (
        P("seq", "head"),
        P("seq", "head"),
        P(),
        P(),
        P(None, "head"),
        P("head"),
        P(None, "head"),
        P(None, "head"),
        P("head"),
        P("head"),
        P("head"),
        P("head", None),
        P(),
        P(),
        P(),
        P(None, "head"),
        P("head"),
        P("head", None),
        P(),
    )
    return jax.shard_map(shards, mesh=mesh, in_specs=in_specs, out_specs=out_specs, check_vma=False)
```

time: 852 us -> 564 us (0.66)
  waiting for transfers between devices: 482 us -> 349 us
  matrix products: 120 us -> 31.7 us
  other arithmetic: 95.7 us -> 29.1 us
  local copies, waits for them, and re-layouts: 48.5 us -> 21.5 us
  starting transfers between devices: 0.58 us -> 26.5 us
  Pallas kernels: 0 us -> 12.3 us
    reduce_scatter x1 -> x0, waiting for transfers between devices: 103 us -> none  [shards(): lax.psum_scatter(key_terms, 'seq', scatter_dimension=0, tiled=True)]
    dot_general x14 -> x0, matrix products: 88 us -> none  [the longest x2 24.9 us: score_parts(): jnp.einsum('hqd,khd->hqk', query_blk, key_blk, preferred_element_type=jnp...]
    all_gather x2 -> x0, waiting for transfers between devices: 85.4 us -> none  [the longest x1 43.9 us: shards(): lax.all_gather(key_rows, 'seq', axis=0, tiled=True)]
    ppermute x0 -> x16, waiting for transfers between devices: none -> 47 us  [the longest x3 9.1 us: ring_scatter(): a = lax.ppermute(a, 'seq', FWD)]
    reduce_sum x14 -> x5, other arithmetic: 37.8 us -> 3.11 us  [the longest x1 1.97 us: shards(): grad_sub_gain = jnp.sum(grad_sub * centered, axis=0)]
    ppermute x0 -> x16, starting transfers between devices: none -> 26.3 us  [the longest x3 10.6 us: ring_scatter(): a = lax.ppermute(a, 'seq', FWD)]
    reduce_scatter x1, waiting for transfers between devices: 11.9 us -> 30.2 us  [shards(): lax.psum_scatter(jnp.dot(sub_out, w_out, preferred_element_type=jnp.float...]
    and x4 -> x0, other arithmetic: 16.5 us -> none  [pattern_count(): allowed & (query_place[:, None] // seg_width == key_place[None, :] // seg...]
  transfers between devices with their start and end apart: 8 -> 21, of which waited for: 8 -> 16; matrix products, arithmetic and copies ran while one was open for 5% -> 8% of each run, Pallas kernels for 0% -> 0%
where the time goes in v1:
time: 564 us; the launch traced here: 563 us
  waiting for transfers between devices  349 us (62%)
  blocking collectives  78.3 us (14%)
  matrix products  31.7 us (6%)
  other arithmetic  29.1 us (5%)
  starting transfers between devices  26.5 us (5%)
  local copies, waits for them, and re-layouts  21.5 us (4%)
  between operations  14.8 us (3%)
  Pallas kernels  12.3 us (2%)
    psum x1, waiting for transfers between devices, shards(): lax.psum((grad_ln1_gain, grad_ln1_bias, grad_w_query, grad_b_query, grad_...  201 us
    psum x1, blocking collectives, shards(): lax.psum((grad_ln1_gain, grad_ln1_bias, grad_w_query, grad_b_query, grad_...  39.4 us
    psum x1, waiting for transfers between devices, shards(): lax.psum(jnp.dot(grad_inner, w_up.T, preferred_element_type=jnp.float32)....  35.1 us
    psum x1, waiting for transfers between devices, shards(): lax.psum(grad_normed.astype(jnp.bfloat16), 'head').astype(jnp.float32)  35 us
    reduce_scatter x1, waiting for transfers between devices, shards(): lax.psum_scatter(jnp.dot(sub_out, w_out, preferred_element_type=jnp.float...  30.2 us
    unnamed x145, local copies, waits for them, and re-layouts  15.1 us
  transfers between devices with their start and end apart: 21, of which 16 were waited for; matrix products, arithmetic and copies ran while one was open for 8% of the time, Pallas kernels for 0%

profile of v1, /device:TPU:0, one launch (start us, length us, event | category | flops | bytes accessed | tf_op | source)
XLA Modules:
  0.0 563.2 jit_solution(16136823421500424242)
XLA Ops:
  7.3 10.4 %all_gather.9 = bf16[512,768]{0,1:T(8,128)(2,1)S(1)} all-gather(bf16[512,192]{0,1:T(8,128)(2,1)} %param.31), channel_id=1, replica_groups=mesh['seq'=8,'head'=4] {'head'}, dimensions={1}, use_global_device_ids=true | all-gather | bytes 983040 | tf_op jit(solution)/shard_map/all_gather | solution.py:212
  20.7 1.6 collective-permute-start
  26.1 5.6 or_convert_fusion.fq.fk
  34.4 1.4 fusion.28.q
  35.8 1.6 collective-permute-start.2
  37.9 1.1 bitcast_dynamic-update-slice_fusion.5
  38.9 1.1 bitcast_dynamic-update-slice_fusion.4
  40.0 6.9 %collective-permute-done.2 = bf16[512,384]{1,0:T(8,128)(2,1)S(1)} collective-permute-done((bf16[512,384]{1,0:T(8,128)(2,1)}, bf16[512,384]{1,0:T(8,128)(2,1)S(1)}, u32[]{:S(2)}, u32[]{:S(2)}) %collective-permute-start.2) | collective-permute-done | bytes 393248 | tf_op jit(solution)/shard_map/ppermute | solution.py:161
  46.8 1.6 collective-permute-start.4
  49.0 9.1 %collective-permute-done.5 = bf16[512,384]{1,0:T(8,128)(2,1)S(1)} collective-permute-done((bf16[512,384]{1,0:T(8,128)(2,1)S(1)}, bf16[512,384]{1,0:T(8,128)(2,1)S(1)}, u32[]{:S(2)}, u32[]{:S(2)}) %collective-permute-start.5) | collective-permute-done | bytes 393248 | tf_op jit(solution)/shard_map/ppermute | solution.py:161
  58.6 1.6 collective-permute-start.6
  60.4 3.4 collective-permute-done.7
  64.5 3.8 attend_fwd.1
  68.5 5.7 %all-reduce.3 = (f32[512]{0:T(512)S(1)}, f32[512]{0:T(512)S(1)}) all-reduce(f32[512]{0:T(512)S(1)} %get-tuple-element.38, f32[512]{0:T(512)S(1)} %get-tuple-element.37), channel_id=1, replica_groups=mesh['seq'=8,'head'=4] {'head'}, use_global_device_ids=true, to_apply=%region_16.17 | all-reduce | flops 1024 | bytes 8192 | tf_op jit(solution)/shard_map/psum | solution.py:234
  74.2 2.5 convolution_convert_fusion.2
  77.5 8.7 %all_gather.11 = bf16[512,768]{0,1:T(8,128)(2,1)} all-gather(bf16[512,192]{0,1:T(8,128)(2,1)S(1)} %copy-done.34), channel_id=1, replica_groups=mesh['seq'=8,'head'=4] {'head'}, dimensions={1}, use_global_device_ids=true | all-gather | bytes 983040 | tf_op jit(solution)/shard_map/all_gather | solution.py:263
  86.2 30.2 %reduce-scatter.3.cloned.1.call-done = bf16[512,192]{0,1:T(8,128)(2,1)} async-done(((bf16[512,768]{0,1:T(8,128)(2,1)}), bf16[512,192]{0,1:T(8,128)(2,1)}) %reduce-scatter.3.cloned.1.call-update) | async-done | bytes 196624 | tf_op jit(solution)/shard_map/reduce_scatter | solution.py:241
  116.4 1.1 fusion.39
  117.6 8.4 %all_gather.10 = bf16[512,768]{0,1:T(8,128)(2,1)S(1)} all-gather(bf16[512,192]{0,1:T(8,128)(2,1)S(1)} %fusion.39), channel_id=1, replica_groups=mesh['seq'=8,'head'=4] {'head'}, dimensions={1}, use_global_device_ids=true | all-gather | bytes 983040 | tf_op jit(solution)/shard_map/all_gather | solution.py:249
  126.8 1.1 convolution_add_fusion
  128.0 5.8 %convert_reduce_fusion.5 = (f32[768]{0:T(1024)}, bf16[512,768]{1,0:T(8,128)(2,1)S(1)}, f32[512,768]{1,0:T(8,128)}) fusion(f32[512,768]{1,0:T(8,128)S(1)} %convolution_add_fusion, bf16[512,768]{0,1:T(8,128)(2,1)S(1)} %copy-done.15, bf16[768,768]{1,0:T(8,128)(2,1)S(1)} %copy-done), kind=kOutput, calls=%fused_computation.40 | convolution fusion | flops 633076992 | bytes 5901312 | tf_op jit(solution)/shard_map/dot_general | solution.py:267
  134.8 1.7 convolution_convert_fusion
  136.6 35.1 %all-reduce.8.cloned.1.call-done = bf16[512,768]{0,1:T(8,128)(2,1)} async-done(((bf16[512,768]{0,1:T(8,128)(2,1)}), bf16[512,768]{0,1:T(8,128)(2,1)}) %all-reduce.8.cloned.1.call-update) | async-done | bytes 786448 | tf_op jit(solution)/shard_map/psum | solution.py:272
  171.7 2.1 convert_reduce_fusion.1
  174.8 1.1 convert_reduce_fusion.6
  175.9 1.2 copy-done.12
  177.0 1.6 fusion.79
  178.7 2.0 copy.79
  180.7 2.0 multiply_reduce_fusion
  182.6 5.8 %all-reduce.2 = (f32[512]{0:T(512)S(1)}, f32[512]{0:T(512)S(1)}) all-reduce(f32[512]{0:T(512)S(1)} %get-tuple-element.32, f32[512]{0:T(512)S(1)} %get-tuple-element.36), channel_id=1, replica_groups=mesh['seq'=8,'head'=4] {'head'}, use_global_device_ids=true, to_apply=%region_27.28 | all-reduce | flops 1024 | bytes 8192 | tf_op jit(solution)/shard_map/psum | solution.py:285
  188.4 1.4 multiply_convert_fusion.1.do
  189.8 8.5 %attend_bwd.1 = (bf16[512,192]{1,0:T(8,128)(2,1)S(1)}, bf16[8,512,384]{2,1,0:T(8,128)(2,1)S(1)}) custom-call(s32[10]{0:T(128)S(1)} %pad_add_fusion.sc, bf16[512,192]{1,0:T(8,128)(2,1)S(1)} %fusion.28.q, bf16[4096,128]{1,0:T(8,128)(2,1)S(1)} %or_convert_fusion.fq.fk, bf16[512,192]{1,0:T(8,128)(2,1)S(1)} %multiply_convert_fusion.1.do, ...), custom_call_target="tpu_custom_call" | custom-call | tf_op jit(solution)/shard_map/attend_bwd/pallas_call | solution.py:150
  198.4 7.3 %collective-permute-start.8 = (bf16[256,384]{1,0:T(8,128)(2,1)S(1)}, bf16[256,384]{1,0:T(8,128)(2,1)S(1)}, u32[]{:S(2)}, u32[]{:S(2)}) collective-permute-start(bf16[256,384]{1,0:T(8,128)(2,1)S(1)} %get-tuple-element.81), channel_id=1, source_target_pairs={{0,8},{8,16},{16,24},{24,28},{28,20},{20,12},{12,4},{4,0},{1,9},{9... | collective-permute-start | bytes 589832 | tf_op jit(solution)/shard_map/ppermute | solution.py:173
  205.7 3.9 collective-permute-done.8
  209.6 7.6 %collective-permute-done.12 = bf16[256,384]{1,0:T(8,128)(2,1)S(1)} collective-permute-done((bf16[256,384]{1,0:T(8,128)(2,1)S(1)}, bf16[256,384]{1,0:T(8,128)(2,1)S(1)}, u32[]{:S(2)}, u32[]{:S(2)}) %collective-permute-start.12) | collective-permute-done | bytes 196640 | tf_op jit(solution)/shard_map/ppermute | solution.py:173
  217.4 5.4 collective-permute-start.9
  223.1 6.8 %collective-permute-done.9 = bf16[512,384]{1,0:T(8,128)(2,1)S(1)} collective-permute-done((bf16[512,384]{1,0:T(8,128)(2,1)S(1)}, bf16[512,384]{1,0:T(8,128)(2,1)S(1)}, u32[]{:S(2)}, u32[]{:S(2)}) %collective-permute-start.9) | collective-permute-done | bytes 393248 | tf_op jit(solution)/shard_map/ppermute | solution.py:175
  230.1 2.8 collective-permute-start.10
  232.8 2.2 fusion.85
  235.1 2.3 fusion.73
  237.4 1.7 collective-permute-done.10
  240.0 1.8 convolution_convert_fusion.1
  241.9 2.6 fusion.80
  244.5 2.5 collective-permute-start.11
  247.0 1.9 collective-permute-done.14
  248.9 1.2 fusion.32
  250.2 1.2 fusion.82
  251.5 1.4 fusion.69
  253.4 4.6 collective-permute-done.15
  258.1 1.1 fusion.35
  259.6 1.5 fusion.81
  261.1 1.4 add_convert_fusion
  262.5 1.2 fusion.83
  263.8 1.2 fusion.84
  266.7 1.8 add_convert_fusion.3
  268.6 35.0 %all-reduce.10.cloned.1.call-done = bf16[512,768]{0,1:T(8,128)(2,1)} async-done(((bf16[512,768]{0,1:T(8,128)(2,1)}), bf16[512,768]{0,1:T(8,128)(2,1)}) %all-reduce.10.cloned.1.call-update) | async-done | bytes 786448 | tf_op jit(solution)/shard_map/psum | solution.py:309
  303.7 2.0 fusion.22
  305.7 39.4 %all-reduce = (f32[768]{0:T(1024)}, f32[768]{0:T(1024)}, f32[192]{0:T(256)}, f32[192]{0:T(256)}, f32[192]{0:T(256)}, /*index=5*/f32[192]{0:T(256)}, f32[768]{0:T...) all-reduce(f32[768]{0:T(1024)S(1)} %get-tuple-element.29, ...), channel_id=1, replica_groups=mesh['seq'=8,'head'=4] {'seq'}, use_global_device_ids=true, to_apply=%region_32.33 | all-reduce | flops 6144 | bytes 49152 | tf_op jit(solution)/shard_map/psum | solution.py:314
  345.6 1.8 dynamic-slice_add_fusion
  347.5 200.7 %all-reduce.12.cloned.1.call-done = (f32[768,192]{0,1:T(8,128)}, f32[768,192]{0,1:T(8,128)}, f32[768,192]{0,1:T(8,128)}, f32[192,768]{1,0:T(8,128)}, f32[768,768]{1,0:T(8,128)}, /*index=5*/f32[768,768]{1,0:T(8,128)}) async-done(((f32[768,192]{0,1:T(8,128)}, f32[768,192]{0,1:T(8,128)}, f32[768,192]{0,1:T(8,128)}, f32[192,768]{1,0:T(8,128)}, f32[768,768]{1,0:T(8,128)}, /*index=5*/f32[768,768]{1,0:T(8,128)}), ...) | async-done | bytes 7077904 | tf_op jit(solution)/shard_map/psum | solution.py:314
  548.2 2.0 copy.105
  552.7 1.4 copy.109
  554.1 1.1 copy-done.20
  555.2 1.4 copy.110
  (217 shorter events, 22.9 us)
Async XLA Ops:
  7.2 120.8 %copy-start = (bf16[768,768]{1,0:T(8,128)(2,1)S(1)}, bf16[768,768]{1,0:T(8,128)(2,1)}, u32[]{:S(2)}) copy-start(bf16[768,768]{1,0:T(8,128)(2,1)} %param.47) | copy-start | bytes 3538948
  7.2 10.9 %copy-start.39 = (f32[768]{0:T(1024)S(1)}, f32[768]{0:T(1024)}, u32[]{:S(2)}) copy-start(f32[768]{0:T(1024)} %param.33) | copy-start | bytes 9220
  7.2 10.9 %copy-start.36 = (f32[768]{0:T(1024)S(1)}, f32[768]{0:T(1024)}, u32[]{:S(2)}) copy-start(f32[768]{0:T(1024)} %param.32) | copy-start | bytes 9220
  7.2 109.2 %reduce-scatter.3.cloned.1.call-start = ((), (), s32[]{:S(2)}) async-start(), calls=%async_computation.2 | async-start | bytes 983040 | tf_op jit(solution)/shard_map/reduce_scatter | solution.py:241
  19.2 4.1 copy-start.63
  19.2 5.5 copy-start.38
  19.2 5.5 copy-start.43
  19.2 6.2 %copy-start.62 = (pred[3,128]{1,0:T(4,128)(4,1)S(1)}, pred[3,128]{1,0:T(4,128)(4,1)}, u32[]{:S(2)}) copy-start(pred[3,128]{1,0:T(4,128)(4,1)} %constant.367.clone) | copy-start | bytes 1156
  19.2 6.6 %copy-start.53 = (pred[128]{0:T(512)(128)(4,1)S(1)}, pred[128]{0:T(512)(128)(4,1)}, u32[]{:S(2)}) copy-start(pred[128]{0:T(512)(128)(4,1)} %constant.370.clone) | copy-start | bytes 388
  19.2 6.6 %copy-start.54 = (pred[128]{0:T(512)(128)(4,1)S(1)}, pred[128]{0:T(512)(128)(4,1)}, u32[]{:S(2)}) copy-start(pred[128]{0:T(512)(128)(4,1)} %constant.372.clone) | copy-start | bytes 388
  19.2 6.6 %copy-start.55 = (pred[128]{0:T(512)(128)(4,1)S(1)}, pred[128]{0:T(512)(128)(4,1)}, u32[]{:S(2)}) copy-start(pred[128]{0:T(512)(128)(4,1)} %constant.373.clone) | copy-start | bytes 388
  19.3 6.6 %copy-start.56 = (pred[128]{0:T(512)(128)(4,1)S(1)}, pred[128]{0:T(512)(128)(4,1)}, u32[]{:S(2)}) copy-start(pred[128]{0:T(512)(128)(4,1)} %constant.371.clone) | copy-start | bytes 388
  19.6 6.4 %copy-start.47 = (s32[128]{0:T(128)S(1)}, s32[128]{0:T(128)}, u32[]{:S(2)}) copy-start(s32[128]{0:T(128)} %constant.382) | copy-start | bytes 1540
  19.6 6.4 %copy-start.48 = (s32[128]{0:T(128)S(1)}, s32[128]{0:T(128)}, u32[]{:S(2)}) copy-start(s32[128]{0:T(128)} %constant.381) | copy-start | bytes 1540
  19.6 6.4 %copy-start.49 = (s32[128]{0:T(128)S(1)}, s32[128]{0:T(128)}, u32[]{:S(2)}) copy-start(s32[128]{0:T(128)} %constant.380) | copy-start | bytes 1540
  19.6 6.4 %copy-start.50 = (s32[128]{0:T(128)S(1)}, s32[128]{0:T(128)}, u32[]{:S(2)}) copy-start(s32[128]{0:T(128)} %constant.379) | copy-start | bytes 1540
  19.7 6.4 %copy-start.51 = (s32[128]{0:T(128)S(1)}, s32[128]{0:T(128)}, u32[]{:S(2)}) copy-start(s32[128]{0:T(128)} %constant.376) | copy-start | bytes 1540
  19.7 6.4 %copy-start.52 = (pred[128]{0:T(512)(128)(4,1)S(1)}, pred[128]{0:T(512)(128)(4,1)}, u32[]{:S(2)}) copy-start(pred[128]{0:T(512)(128)(4,1)} %constant.378) | copy-start | bytes 388
  20.7 15.1 %collective-permute-start = (bf16[512,384]{1,0:T(8,128)(2,1)}, bf16[512,384]{1,0:T(8,128)(2,1)}, u32[]{:S(2)}, u32[]{:S(2)}) collective-permute-start(bf16[512,384]{1,0:T(8,128)(2,1)} %copy.75), channel_id=1, source_target_pairs={{0,8},{8,16},{16,24},{24,28},{28,20},{20,12},{12,4},{4,0},{1,9},{9... | collective-permute-start | bytes 1179656 | tf_op jit(solution)/shard_map/ppermute | solution.py:161
  22.2 15.2 %collective-permute-start.1 = (bf16[512,384]{1,0:T(8,128)(2,1)}, bf16[512,384]{1,0:T(8,128)(2,1)}, u32[]{:S(2)}, u32[]{:S(2)}) collective-permute-start(bf16[512,384]{1,0:T(8,128)(2,1)} %copy.75), channel_id=1, source_target_pairs={{8,0},{16,8},{24,16},{28,24},{20,28},{12,20},{4,12},{0,4},{9,1},{1... | collective-permute-start | bytes 1179656 | tf_op jit(solution)/shard_map/ppermute | solution.py:161
  25.8 8.5 %copy-start.5 = (bf16[512,768]{0,1:T(8,128)(2,1)S(1)}, bf16[512,768]{0,1:T(8,128)(2,1)}, u32[]{:S(2)}) copy-start(bf16[512,768]{0,1:T(8,128)(2,1)} %copy-done.4) | copy-start | bytes 2359300
  25.8 8.5 %copy-start.61 = (f32[192]{0:T(256)S(1)}, f32[192]{0:T(256)}, u32[]{:S(2)}) copy-start(f32[192]{0:T(256)} %param.35) | copy-start | bytes 2308
  35.8 11.1 %collective-permute-start.2 = (bf16[512,384]{1,0:T(8,128)(2,1)}, bf16[512,384]{1,0:T(8,128)(2,1)S(1)}, u32[]{:S(2)}, u32[]{:S(2)}) collective-permute-start(bf16[512,384]{1,0:T(8,128)(2,1)} %collective-permute-done), channel_id=1, source_target_pairs={{0,8},{8,16},{16,24},{24,28},{28,20},{20,12},{12,4},{4,0},{1,9},{9... | collective-permute-start | bytes 1179656 | tf_op jit(solution)/shard_map/ppermute | solution.py:161
  37.4 11.0 %collective-permute-start.3 = (bf16[512,384]{1,0:T(8,128)(2,1)}, bf16[512,384]{1,0:T(8,128)(2,1)S(1)}, u32[]{:S(2)}, u32[]{:S(2)}) collective-permute-start(bf16[512,384]{1,0:T(8,128)(2,1)} %collective-permute-done.1), channel_id=1, source_target_pairs={{8,0},{16,8},{24,16},{28,24},{20,28},{12,20},{4,12},{0,4},{9,1},{1... | collective-permute-start | bytes 1179656 | tf_op jit(solution)/shard_map/ppermute | solution.py:161
  46.8 11.8 %collective-permute-start.4 = (bf16[512,384]{1,0:T(8,128)(2,1)S(1)}, bf16[512,384]{1,0:T(8,128)(2,1)S(1)}, u32[]{:S(2)}, u32[]{:S(2)}) collective-permute-start(bf16[512,384]{1,0:T(8,128)(2,1)S(1)} %collective-permute-done.2), channel_id=1, source_target_pairs={{0,8},{8,16},{16,24},{24,28},{28,20},{20,12},{12,4},{4,0},{1,9},{9... | collective-permute-start | bytes 1179656 | tf_op jit(solution)/shard_map/ppermute | solution.py:161
  48.4 9.7 %collective-permute-start.5 = (bf16[512,384]{1,0:T(8,128)(2,1)S(1)}, bf16[512,384]{1,0:T(8,128)(2,1)S(1)}, u32[]{:S(2)}, u32[]{:S(2)}) collective-permute-start(bf16[512,384]{1,0:T(8,128)(2,1)S(1)} %collective-permute-done.3), channel_id=1, source_target_pairs={{8,0},{16,8},{24,16},{28,24},{20,28},{12,20},{4,12},{0,4},{9,1},{1... | collective-permute-start | bytes 1179656 | tf_op jit(solution)/shard_map/ppermute | solution.py:161
  58.1 5.7 %collective-permute-start.7 = (bf16[256,384]{1,0:T(8,128)(2,1)S(1)}, bf16[256,384]{1,0:T(8,128)(2,1)S(1)}, u32[]{:S(2)}, u32[]{:S(2)}) collective-permute-start(bf16[256,384]{1,0:T(8,128)(2,1)S(1)} %slice.91), channel_id=1, source_target_pairs={{8,0},{16,8},{24,16},{28,24},{20,28},{12,20},{4,12},{0,4},{9,1},{1... | collective-permute-start | bytes 589832 | tf_op jit(solution)/shard_map/ppermute | solution.py:162
  58.6 5.7 %collective-permute-start.6 = (bf16[256,384]{1,0:T(8,128)(2,1)S(1)}, bf16[256,384]{1,0:T(8,128)(2,1)S(1)}, u32[]{:S(2)}, u32[]{:S(2)}) collective-permute-start(bf16[256,384]{1,0:T(8,128)(2,1)S(1)} %slice.90), channel_id=1, source_target_pairs={{0,8},{8,16},{16,24},{24,28},{28,20},{20,12},{12,4},{4,0},{1,9},{9... | collective-permute-start | bytes 589832 | tf_op jit(solution)/shard_map/ppermute | solution.py:162
  64.4 9.7 %copy-start.37 = (f32[192]{0:T(256)S(1)}, f32[192]{0:T(256)}, u32[]{:S(2)}) copy-start(f32[192]{0:T(256)} %param.39) | copy-start | bytes 2308
  64.4 9.7 %copy-start.40 = (f32[192]{0:T(256)S(1)}, f32[192]{0:T(256)}, u32[]{:S(2)}) copy-start(f32[192]{0:T(256)} %param.40) | copy-start | bytes 2308
  68.3 9.2 %copy-start.34 = (bf16[512,192]{0,1:T(8,128)(2,1)S(1)}, bf16[512,192]{0,1:T(8,128)(2,1)}, u32[]{:S(2)}) copy-start(bf16[512,192]{0,1:T(8,128)(2,1)} %param.49) | copy-start | bytes 589828
  74.2 42.2 %copy-start.22 = (bf16[512,192]{0,1:T(8,128)(2,1)S(1)}, bf16[512,192]{0,1:T(8,128)(2,1)}, u32[]{:S(2)}) copy-start(bf16[512,192]{0,1:T(8,128)(2,1)} %param.31) | copy-start | bytes 589828
  76.7 95.0 %all-reduce.8.cloned.1.call-start = ((), (), s32[]{:S(2)}) async-start(), calls=%async_computation.4 | async-start | bytes 1572864 | tf_op jit(solution)/shard_map/psum | solution.py:272
  86.2 40.7 %copy-start.35 = (f32[768]{0:T(1024)S(1)}, f32[768]{0:T(1024)}, u32[]{:S(2)}) copy-start(f32[768]{0:T(1024)} %param.43) | copy-start | bytes 9220
  86.2 40.7 %copy-start.58 = (f32[768]{0:T(1024)S(1)}, f32[768]{0:T(1024)}, u32[]{:S(2)}) copy-start(f32[768]{0:T(1024)} %param.46) | copy-start | bytes 9220
  86.2 40.7 %copy-start.59 = (f32[768]{0:T(1024)S(1)}, f32[768]{0:T(1024)}, u32[]{:S(2)}) copy-start(f32[768]{0:T(1024)} %param.44) | copy-start | bytes 9220
  116.4 10.4 %copy-start.57 = (bf16[768,768]{1,0:T(8,128)(2,1)S(1)}, bf16[768,768]{1,0:T(8,128)(2,1)}, u32[]{:S(2)}) copy-start(bf16[768,768]{1,0:T(8,128)(2,1)} %param.45) | copy-start | bytes 3538948
  128.0 5.8 %copy-start.23 = (f32[512,768]{1,0:T(8,128)}, f32[512,768]{1,0:T(8,128)S(1)}, u32[]{:S(2)}) copy-start(f32[512,768]{1,0:T(8,128)S(1)} %convolution_add_fusion) | copy-start | bytes 4718596
  136.5 130.2 %reduce-scatter.5.cloned.1.call-start = ((), (), s32[]{:S(2)}) async-start(), calls=%async_computation.3 | async-start | bytes 983040 | tf_op jit(solution)/shard_map/reduce_scatter | solution.py:255
  198.3 40.8 %copy-start.2 = (bf16[8,512,384]{2,1,0:T(8,128)(2,1)}, bf16[8,512,384]{2,1,0:T(8,128)(2,1)S(1)}, u32[]{:S(2)}) copy-start(bf16[8,512,384]{2,1,0:T(8,128)(2,1)S(1)} %get-tuple-element.26) | copy-start | bytes 9437188
  198.3 24.4 %copy-start.24 = (f32[512,768]{1,0:T(8,128)S(1)}, f32[512,768]{1,0:T(8,128)}, u32[]{:S(2)}) copy-start(f32[512,768]{1,0:T(8,128)} %copy-done.23) | copy-start | bytes 4718596
  198.3 24.4 %copy-start.25 = (f32[512,768]{1,0:T(8,128)S(1)}, f32[512,768]{1,0:T(8,128)}, u32[]{:S(2)}) copy-start(f32[512,768]{1,0:T(8,128)} %get-tuple-element.68) | copy-start | bytes 4718596
  198.4 11.2 %collective-permute-start.8 = (bf16[256,384]{1,0:T(8,128)(2,1)S(1)}, bf16[256,384]{1,0:T(8,128)(2,1)S(1)}, u32[]{:S(2)}, u32[]{:S(2)}) collective-permute-start(bf16[256,384]{1,0:T(8,128)(2,1)S(1)} %get-tuple-element.81), channel_id=1, source_target_pairs={{0,8},{8,16},{16,24},{24,28},{28,20},{20,12},{12,4},{4,0},{1,9},{9... | collective-permute-start | bytes 589832 | tf_op jit(solution)/shard_map/ppermute | solution.py:173
  205.7 11.5 %collective-permute-start.12 = (bf16[256,384]{1,0:T(8,128)(2,1)S(1)}, bf16[256,384]{1,0:T(8,128)(2,1)S(1)}, u32[]{:S(2)}, u32[]{:S(2)}) collective-permute-start(bf16[256,384]{1,0:T(8,128)(2,1)S(1)} %get-tuple-element.82), channel_id=1, source_target_pairs={{8,0},{16,8},{24,16},{28,24},{20,28},{12,20},{4,12},{0,4},{9,1},{1... | collective-permute-start | bytes 589832 | tf_op jit(solution)/shard_map/ppermute | solution.py:173
  217.4 12.6 %collective-permute-start.9 = (bf16[512,384]{1,0:T(8,128)(2,1)S(1)}, bf16[512,384]{1,0:T(8,128)(2,1)S(1)}, u32[]{:S(2)}, u32[]{:S(2)}) collective-permute-start(bf16[512,384]{1,0:T(8,128)(2,1)S(1)} %pad_maximum_fusion.1), channel_id=1, source_target_pairs={{0,8},{8,16},{16,24},{24,28},{28,20},{20,12},{12,4},{4,0},{1,9},{9... | collective-permute-start | bytes 1179656 | tf_op jit(solution)/shard_map/ppermute | solution.py:175
  223.0 9.9 %copy-start.17 = (bf16[512,768]{0,1:T(8,128)(2,1)S(1)}, bf16[512,768]{0,1:T(8,128)(2,1)}, u32[]{:S(2)}) copy-start(bf16[512,768]{0,1:T(8,128)(2,1)} %all_gather.11) | copy-start | bytes 2359300
  223.0 14.4 %collective-permute-start.13 = (bf16[512,384]{1,0:T(8,128)(2,1)S(1)}, bf16[512,384]{1,0:T(8,128)(2,1)S(1)}, u32[]{:S(2)}, u32[]{:S(2)}) collective-permute-start(bf16[512,384]{1,0:T(8,128)(2,1)S(1)} %pad_maximum_fusion.2), channel_id=1, source_target_pairs={{8,0},{16,8},{24,16},{28,24},{20,28},{12,20},{4,12},{0,4},{9,1},{1... | collective-permute-start | bytes 1179656 | tf_op jit(solution)/shard_map/ppermute | solution.py:175
  230.0 5.0 copy-start.9
  230.1 5.0 copy-start.60
  230.1 5.0 copy-start.65
  230.1 9.0 %collective-permute-start.10 = (bf16[512,384]{1,0:T(8,128)(2,1)S(1)}, bf16[512,384]{1,0:T(8,128)(2,1)S(1)}, u32[]{:S(2)}, u32[]{:S(2)}) collective-permute-start(bf16[512,384]{1,0:T(8,128)(2,1)S(1)} %fusion.33), channel_id=1, source_target_pairs={{0,8},{8,16},{16,24},{24,28},{28,20},{20,12},{12,4},{4,0},{1,9},{9... | collective-permute-start | bytes 1179656 | tf_op jit(solution)/shard_map/ppermute | solution.py:177
  240.0 8.9 %collective-permute-start.14 = (bf16[512,384]{1,0:T(8,128)(2,1)}, bf16[512,384]{1,0:T(8,128)(2,1)}, u32[]{:S(2)}, u32[]{:S(2)}) collective-permute-start(bf16[512,384]{1,0:T(8,128)(2,1)} %get-tuple-element.78), channel_id=1, source_target_pairs={{8,0},{16,8},{24,16},{28,24},{20,28},{12,20},{4,12},{0,4},{9,1},{1... | collective-permute-start | bytes 1179656 | tf_op jit(solution)/shard_map/ppermute | solution.py:177
  241.9 61.8 %all-reduce.10.cloned.1.call-start = ((), (), s32[]{:S(2)}) async-start(), calls=%async_computation.5 | async-start | bytes 1572864 | tf_op jit(solution)/shard_map/psum | solution.py:309
  241.9 8.3 %copy-start.6 = (bf16[512,768]{0,1:T(8,128)(2,1)S(1)}, bf16[512,768]{0,1:T(8,128)(2,1)}, u32[]{:S(2)}) copy-start(bf16[512,768]{0,1:T(8,128)(2,1)} %copy-done.4) | copy-start | bytes 2359300
  244.5 6.9 %copy-start.13 = (f32[512,768]{0,1:T(8,128)S(1)}, f32[512,768]{0,1:T(8,128)}, u32[]{:S(2)}) copy-start(f32[512,768]{0,1:T(8,128)} %copy-done.12) | copy-start | bytes 4718596
  244.5 6.9 %copy-start.41 = (f32[192]{0:T(256)S(1)}, f32[192]{0:T(256)}, u32[]{:S(2)}) copy-start(f32[192]{0:T(256)} %param.40) | copy-start | bytes 2308
  244.5 8.9 %collective-permute-start.11 = (bf16[512,384]{1,0:T(8,128)(2,1)S(1)}, bf16[512,384]{1,0:T(8,128)(2,1)S(1)}, u32[]{:S(2)}, u32[]{:S(2)}) collective-permute-start(bf16[512,384]{1,0:T(8,128)(2,1)S(1)} %get-tuple-element.77), channel_id=1, source_target_pairs={{0,8},{8,16},{16,24},{24,28},{28,20},{20,12},{12,4},{4,0},{1,9},{9... | collective-permute-start | bytes 1179656 | tf_op jit(solution)/shard_map/ppermute | solution.py:179
  250.1 7.9 %collective-permute-start.15 = (bf16[512,384]{1,0:T(8,128)(2,1)S(1)}, bf16[512,384]{1,0:T(8,128)(2,1)S(1)}, u32[]{:S(2)}, u32[]{:S(2)}) collective-permute-start(bf16[512,384]{1,0:T(8,128)(2,1)S(1)} %fusion.32), channel_id=1, source_target_pairs={{8,0},{16,8},{24,16},{28,24},{20,28},{12,20},{4,12},{0,4},{9,1},{1... | collective-permute-start | bytes 1179656 | tf_op jit(solution)/shard_map/ppermute | solution.py:179
  262.5 285.7 %all-reduce.12.cloned.1.call-start = ((), (), s32[]{:S(2)}) async-start(), calls=%async_computation.6 | async-start | bytes 14155776 | tf_op jit(solution)/shard_map/psum | solution.py:314
  265.0 38.6 %copy-start.11 = (bf16[512,768]{0,1:T(8,128)(2,1)S(1)}, bf16[512,768]{0,1:T(8,128)(2,1)}, u32[]{:S(2)}) copy-start(bf16[512,768]{0,1:T(8,128)(2,1)} %copy-done.10) | copy-start | bytes 2359300
  265.0 40.6 %copy-start.42 = (f32[192]{0:T(256)S(1)}, f32[192]{0:T(256)}, u32[]{:S(2)}) copy-start(f32[192]{0:T(256)} %get-tuple-element.106) | copy-start | bytes 2308
  265.0 40.6 %copy-start.44 = (f32[768]{0:T(1024)S(1)}, f32[768]{0:T(1024)}, u32[]{:S(2)}) copy-start(f32[768]{0:T(1024)} %get-tuple-element.66) | copy-start | bytes 9220
  265.0 40.6 %copy-start.45 = (f32[192]{0:T(256)S(1)}, f32[192]{0:T(256)}, u32[]{:S(2)}) copy-start(f32[192]{0:T(256)} %get-tuple-element.31) | copy-start | bytes 2308
  303.7 41.4 %copy-start.19 = (bf16[512,768]{0,1:T(8,128)(2,1)S(1)}, bf16[512,768]{0,1:T(8,128)(2,1)}, u32[]{:S(2)}) copy-start(bf16[512,768]{0,1:T(8,128)(2,1)} %all-reduce.10.cloned.1.call-done) | copy-start | bytes 2359300
  (23 other events, 44.8 us)
Sparse Core Ops, SparseCore 0:
  76.8 39.5 reduce-scatter.2
  136.7 34.9 all-reduce.7
  242.0 24.7 reduce-scatter.4
  269.0 34.6 all-reduce.9
  310.3 237.8 all-reduce.11
